TPU v7x, 512 devices: a whole 4x8x8 slice. The times are simulated.
512 devices in a mesh: leaf: 32 (over z, x), rows: 8 (over y), rhs: 2 (over core).
Axes of the slice: x: 4, y: 8, z: 8, core: 2. Of those that a mesh axis runs over, the one named last changes fastest.
Arguments:
- right_side: float32 [64, 128, 2048], P('leaf', 'rhs', 'rows'), may hold values from -6 to 6
- inverse_diag: bfloat16 [64, 2048, 2048], P('leaf', None, ('rows', 'rhs')), may hold values from -0.1 to 1.5, as said below
- lower_blocks: bfloat16 [64, 16, 128, 2048], P('leaf', None, None, 'rows'), may hold values from -0.0625 to 0.0625
- block_rows: int32 [64, 16], P('leaf'), may hold values from 0 to 79, as said below
Outputs:
- solved: float32 [64, 128, 2048], P('leaf', 'rhs', 'rows')
Inputs may be any that keep to these rules, and one draw needn't show every extreme that they name: `inverse_diag`: in every row of an inverse block, the diagonal entry is positive and larger than every other entry of that row. `block_rows`: row i lists 16 distinct block numbers below 2048 / 128 times the depth of slot i; the first is 0, the first block of the root's rows, and the second is the last block of its parent's rows; the rows of the root and of slot 63 are not read.
All inputs are finite; a program needn't handle non-finite values.
Results may differ from a plain program's by a relative error of at most 0.004.
Values may be sent and summed in bfloat16 or wider, within the bound.
A program may use at most 64 MiB of HBM per device.

v0:
```python
import jax
import jax.numpy as jnp
from jax import lax
from jax.sharding import PartitionSpec as P


def laid_out(pieces, dim):
    dims = list(pieces.shape[1:])
    dims[dim] *= pieces.shape[0]
    return jnp.moveaxis(pieces, 0, dim).reshape(dims)


def from_everyone(x, axis):
    peers = lax.axis_size(axis)
    return lax.all_to_all(jnp.broadcast_to(x[None], (peers, *x.shape)), axis, 0, 0, tiled=True)


def gathered_copies(x, axis, dim):
    return laid_out(from_everyone(x, axis), dim)


def swapped(value, axis, stride):
    mask = 2**stride
    pairs = [(source, source ^ mask) for source in range(lax.axis_size(axis))]
    return lax.ppermute(value, axis, pairs)


def count_divides(number, highest):
    running = jnp.zeros((), jnp.int32)
    for power_index in range(1, highest + 1):
        running = running + (number % 2**power_index == 0).astype(jnp.int32)
    return running


def fold_solve(reduced, inverse_slot, active):
    empty_sum = jnp.zeros((reduced.shape[0], inverse_slot.shape[1]), jnp.float32)
    shard_piece = gathered_copies(reduced, "rows", 1)

    def apply_rows():
        return jnp.dot(shard_piece, inverse_slot, preferred_element_type=jnp.float32)

    return lax.cond(active, apply_rows, lambda: empty_sum)


def local(right_side, inverse_diag, lower_blocks, block_rows):
    leaf_count = lax.axis_size("leaf")
    top_depth = leaf_count.bit_length() - 1
    leaf_index = lax.axis_index("leaf")
    inverse_local = gathered_copies(inverse_diag, "rhs", 2)
    inverse_upper = inverse_local[1]
    depth_upper = top_depth - 1 - count_divides(leaf_index + 1, top_depth)
    block_width = lower_blocks.shape[2]
    rhs_count = right_side.shape[1]
    piece_width = right_side.shape[2]
    ancestors = []
    empty_piece = jnp.zeros((rhs_count, piece_width), jnp.float32)
    solved_upper = jnp.zeros((rhs_count, inverse_upper.shape[1]), jnp.float32)
    solved_lower = empty_piece
    for depth_now in range(top_depth + 1):
        slot_now = 1 if depth_now < top_depth else 0
        if slot_now == 1:
            active = depth_upper == depth_now
        else:
            active = jnp.ones((), jnp.bool_)
        if depth_now > 0:
            joined = jnp.concatenate(ancestors, axis=1)
            slot_rows = block_rows[slot_now]
            slot_weights = lower_blocks[slot_now]

            def apply_offset():
                tile_view = joined.reshape(rhs_count, -1, block_width)
                picked = jnp.take(tile_view, slot_rows, axis=1, mode="clip").reshape(rhs_count, -1)
                weights = slot_weights.reshape(-1, piece_width)
                return jnp.dot(picked, weights, preferred_element_type=jnp.float32)

            offset = lax.cond(active, apply_offset, lambda: empty_piece)
            reduced = (right_side[slot_now] - offset).astype(jnp.bfloat16)
        else:
            reduced = right_side[slot_now].astype(jnp.bfloat16)
        if slot_now == 1:
            result = fold_solve(reduced, inverse_upper, active)
            solved_upper = jnp.where(active, result, solved_upper)
        else:
            solved_lower = fold_solve(reduced, inverse_local[0], active)
        if depth_now < top_depth:
            height = top_depth - depth_now
            sending = solved_upper.astype(jnp.bfloat16)
            arrived = sending
            for bit_number in range(height - 1, -1, -1):
                partner_value = swapped(arrived, "leaf", bit_number)
                if bit_number == height - 1:
                    holder = leaf_index % 2**height == 2 ** (height - 1) - 1
                else:
                    holder = leaf_index % 2 ** (bit_number + 1) == 2 ** (bit_number + 1) - 1
                arrived = jnp.where(holder, arrived, partner_value)
            ancestors.append(gathered_copies(arrived, "rows", 1))
    return jnp.stack([solved_lower, solved_upper])


def solution(mesh):
    return jax.shard_map(
        local,
        mesh=mesh,
        in_specs=(
            P("leaf", "rhs", "rows"),
            P("leaf", None, ("rows", "rhs")),
            P("leaf", None, None, "rows"),
            P("leaf", None),
        ),
        out_specs=P("leaf", "rhs", "rows"),
        check_vma=False,
    )
```

profile of v0, /device:TPU:8, one launch (start us, length us, event | category | flops | bytes accessed | tf_op | source)
XLA Modules:
  0.0 308.6 jit_solution(4177516955153892323)
XLA Ops:
  2.8 3.9 %all-to-all-start.1 = ((bf16[2,2,2048,128]{3,2,1,0:T(8,128)(2,1)}), bf16[2,2,2048,128]{3,2,1,0:T(8,128)(2,1)S(1)}, u32[]{:S(2)}, u32[]{:S(2)}) async-start(bf16[2,2,2048,128]{3,2,1,0:T(8,128)(2,1)} %broadcast_in_dim.47), calls=%async_computation.1 | async-start | bytes 4194304 | tf_op jit(solution)/shard_map/all_to_all | solution.py:15
  10.3 9.1 %all-to-all-start = ((bf16[8,64,256]{2,1,0:T(8,128)(2,1)}), bf16[8,64,256]{2,1,0:T(8,128)(2,1)S(1)}, u32[]{:S(2)}, u32[]{:S(2)}) async-start(bf16[8,64,256]{2,1,0:T(8,128)(2,1)} %broadcast_in_dim.46), calls=%async_computation | async-start | bytes 524288 | tf_op jit(solution)/shard_map/all_to_all | solution.py:15
  24.9 5.5 %all-to-all-done = bf16[8,64,256]{2,1,0:T(8,128)(2,1)S(1)} async-done(((bf16[8,64,256]{2,1,0:T(8,128)(2,1)}), bf16[8,64,256]{2,1,0:T(8,128)(2,1)S(1)}, u32[]{:S(2)}, u32[]{:S(2)}) %all-to-all-start) | async-done | bytes 262176 | tf_op jit(solution)/shard_map/all_to_all | solution.py:15
  30.5 9.1 %collective-permute-start = (bf16[64,256]{1,0:T(8,128)(2,1)S(1)}, bf16[64,256]{1,0:T(8,128)(2,1)S(1)}, u32[]{:S(2)}, u32[]{:S(2)}) collective-permute-start(bf16[64,256]{1,0:T(8,128)(2,1)S(1)} %select_convert_fusion), channel_id=1, source_target_pairs={{0,256},{16,272},{32,288},{48,304},{64,320},{80,336},{96,352},{112... | collective-permute-start | bytes 98312 | tf_op jit(solution)/shard_map/ppermute | solution.py:25
  41.5 4.6 %collective-permute-start.1 = (bf16[64,256]{1,0:T(8,128)(2,1)S(1)}, bf16[64,256]{1,0:T(8,128)(2,1)S(1)}, u32[]{:S(2)}, u32[]{:S(2)}) collective-permute-start(bf16[64,256]{1,0:T(8,128)(2,1)S(1)} %broadcast_select_fusion.7), channel_id=1, source_target_pairs={{0,128},{16,144},{32,160},{48,176},{64,192},{80,208},{96,224},{112... | collective-permute-start | bytes 98312 | tf_op jit(solution)/shard_map/ppermute | solution.py:25
  54.0 4.9 %collective-permute-start.3 = (bf16[64,256]{1,0:T(8,128)(2,1)S(1)}, bf16[64,256]{1,0:T(8,128)(2,1)S(1)}, u32[]{:S(2)}, u32[]{:S(2)}) collective-permute-start(bf16[64,256]{1,0:T(8,128)(2,1)S(1)} %broadcast_select_fusion.10), channel_id=1, source_target_pairs={{0,32},{16,48},{32,0},{48,16},{64,96},{80,112},{96,64},{112,80},{1... | collective-permute-start | bytes 98312 | tf_op jit(solution)/shard_map/ppermute | solution.py:25
  67.9 4.7 %all-to-all-start.2 = ((bf16[8,64,256]{2,1,0:T(8,128)(2,1)}), bf16[8,64,256]{2,1,0:T(8,128)(2,1)S(1)}, u32[]{:S(2)}, u32[]{:S(2)}) async-start(bf16[8,64,256]{2,1,0:T(8,128)(2,1)} %broadcast_in_dim.48), calls=%async_computation.2 | async-start | bytes 524288 | tf_op jit(solution)/shard_map/all_to_all | solution.py:15
  75.3 6.3 %all-to-all-done.2 = bf16[8,64,256]{2,1,0:T(8,128)(2,1)S(1)} async-done(((bf16[8,64,256]{2,1,0:T(8,128)(2,1)}), bf16[8,64,256]{2,1,0:T(8,128)(2,1)S(1)}, u32[]{:S(2)}, u32[]{:S(2)}) %all-to-all-start.2) | async-done | bytes 262176 | tf_op jit(solution)/shard_map/all_to_all | solution.py:15
  82.4 4.8 %all-to-all-start.3 = ((bf16[8,64,256]{2,1,0:T(8,128)(2,1)}), bf16[8,64,256]{2,1,0:T(8,128)(2,1)S(1)}, u32[]{:S(2)}, u32[]{:S(2)}) async-start(bf16[8,64,256]{2,1,0:T(8,128)(2,1)} %broadcast_in_dim.49), calls=%async_computation.3 | async-start | bytes 524288 | tf_op jit(solution)/shard_map/all_to_all | solution.py:15
  87.1 9.1 %all-to-all-done.3 = bf16[8,64,256]{2,1,0:T(8,128)(2,1)S(1)} async-done(((bf16[8,64,256]{2,1,0:T(8,128)(2,1)}), bf16[8,64,256]{2,1,0:T(8,128)(2,1)S(1)}, u32[]{:S(2)}, u32[]{:S(2)}) %all-to-all-start.3) | async-done | bytes 262176 | tf_op jit(solution)/shard_map/all_to_all | solution.py:15
  96.8 4.6 %collective-permute-start.5 = (bf16[64,256]{1,0:T(8,128)(2,1)S(1)}, bf16[64,256]{1,0:T(8,128)(2,1)S(1)}, u32[]{:S(2)}, u32[]{:S(2)}) collective-permute-start(bf16[64,256]{1,0:T(8,128)(2,1)S(1)} %get-tuple-element.131), channel_id=1, source_target_pairs={{0,128},{16,144},{32,160},{48,176},{64,192},{80,208},{96,224},{112... | collective-permute-start | bytes 98312 | tf_op jit(solution)/shard_map/ppermute | solution.py:25
  109.4 4.9 %collective-permute-start.7 = (bf16[64,256]{1,0:T(8,128)(2,1)S(1)}, bf16[64,256]{1,0:T(8,128)(2,1)S(1)}, u32[]{:S(2)}, u32[]{:S(2)}) collective-permute-start(bf16[64,256]{1,0:T(8,128)(2,1)S(1)} %broadcast_select_fusion.9), channel_id=1, source_target_pairs={{0,32},{16,48},{32,0},{48,16},{64,96},{80,112},{96,64},{112,80},{1... | collective-permute-start | bytes 98312 | tf_op jit(solution)/shard_map/ppermute | solution.py:25
  123.2 4.8 %all-to-all-start.4 = ((bf16[8,64,256]{2,1,0:T(8,128)(2,1)}), bf16[8,64,256]{2,1,0:T(8,128)(2,1)S(1)}, u32[]{:S(2)}, u32[]{:S(2)}) async-start(bf16[8,64,256]{2,1,0:T(8,128)(2,1)} %broadcast_in_dim.50), calls=%async_computation.4 | async-start | bytes 524288 | tf_op jit(solution)/shard_map/all_to_all | solution.py:15
  128.0 9.2 %all-to-all-done.4 = bf16[8,64,256]{2,1,0:T(8,128)(2,1)S(1)} async-done(((bf16[8,64,256]{2,1,0:T(8,128)(2,1)}), bf16[8,64,256]{2,1,0:T(8,128)(2,1)S(1)}, u32[]{:S(2)}, u32[]{:S(2)}) %all-to-all-start.4) | async-done | bytes 262176 | tf_op jit(solution)/shard_map/all_to_all | solution.py:15
  140.3 5.6 %all-to-all-start.5 = ((bf16[8,64,256]{2,1,0:T(8,128)(2,1)}), bf16[8,64,256]{2,1,0:T(8,128)(2,1)S(1)}, u32[]{:S(2)}, u32[]{:S(2)}) async-start(bf16[8,64,256]{2,1,0:T(8,128)(2,1)} %broadcast_in_dim.51), calls=%async_computation.5 | async-start | bytes 524288 | tf_op jit(solution)/shard_map/all_to_all | solution.py:15
  145.8 9.1 %all-to-all-done.5 = bf16[8,64,256]{2,1,0:T(8,128)(2,1)S(1)} async-done(((bf16[8,64,256]{2,1,0:T(8,128)(2,1)}), bf16[8,64,256]{2,1,0:T(8,128)(2,1)S(1)}, u32[]{:S(2)}, u32[]{:S(2)}) %all-to-all-start.5) | async-done | bytes 262176 | tf_op jit(solution)/shard_map/all_to_all | solution.py:15
  161.6 5.9 %collective-permute-start.10 = (bf16[64,256]{1,0:T(8,128)(2,1)S(1)}, bf16[64,256]{1,0:T(8,128)(2,1)S(1)}, u32[]{:S(2)}, u32[]{:S(2)}) collective-permute-start(bf16[64,256]{1,0:T(8,128)(2,1)S(1)} %broadcast_select_fusion.5), channel_id=1, source_target_pairs={{0,32},{16,48},{32,0},{48,16},{64,96},{80,112},{96,64},{112,80},{1... | collective-permute-start | bytes 98312 | tf_op jit(solution)/shard_map/ppermute | solution.py:25
  169.4 5.5 %collective-permute-start.11 = (bf16[64,256]{1,0:T(8,128)(2,1)S(1)}, bf16[64,256]{1,0:T(8,128)(2,1)S(1)}, u32[]{:S(2)}, u32[]{:S(2)}) collective-permute-start(bf16[64,256]{1,0:T(8,128)(2,1)S(1)} %broadcast_select_fusion.11), channel_id=1, source_target_pairs={{0,16},{16,0},{32,48},{48,32},{64,80},{80,64},{96,112},{112,96},{1... | collective-permute-start | bytes 98312 | tf_op jit(solution)/shard_map/ppermute | solution.py:25
  177.6 4.8 %all-to-all-start.6 = ((bf16[8,64,256]{2,1,0:T(8,128)(2,1)}), bf16[8,64,256]{2,1,0:T(8,128)(2,1)S(1)}, u32[]{:S(2)}, u32[]{:S(2)}) async-start(bf16[8,64,256]{2,1,0:T(8,128)(2,1)} %broadcast_in_dim.52), calls=%async_computation.6 | async-start | bytes 524288 | tf_op jit(solution)/shard_map/all_to_all | solution.py:15
  182.3 9.8 %all-to-all-done.6 = bf16[8,64,256]{2,1,0:T(8,128)(2,1)S(1)} async-done(((bf16[8,64,256]{2,1,0:T(8,128)(2,1)}), bf16[8,64,256]{2,1,0:T(8,128)(2,1)S(1)}, u32[]{:S(2)}, u32[]{:S(2)}) %all-to-all-start.6) | async-done | bytes 262176 | tf_op jit(solution)/shard_map/all_to_all | solution.py:15
  196.0 5.4 %all-to-all-start.7 = ((bf16[8,64,256]{2,1,0:T(8,128)(2,1)}), bf16[8,64,256]{2,1,0:T(8,128)(2,1)}, u32[]{:S(2)}, u32[]{:S(2)}) async-start(bf16[8,64,256]{2,1,0:T(8,128)(2,1)} %broadcast_in_dim.54), calls=%async_computation.7 | async-start | bytes 524288 | tf_op jit(solution)/shard_map/all_to_all | solution.py:15
  201.4 9.2 %all-to-all-done.7 = bf16[8,64,256]{2,1,0:T(8,128)(2,1)} async-done(((bf16[8,64,256]{2,1,0:T(8,128)(2,1)}), bf16[8,64,256]{2,1,0:T(8,128)(2,1)}, u32[]{:S(2)}, u32[]{:S(2)}) %all-to-all-start.7) | async-done | bytes 262176 | tf_op jit(solution)/shard_map/all_to_all | solution.py:15
  212.7 5.7 %collective-permute-start.12 = (bf16[64,256]{1,0:T(8,128)(2,1)}, bf16[64,256]{1,0:T(8,128)(2,1)}, u32[]{:S(2)}, u32[]{:S(2)}) collective-permute-start(bf16[64,256]{1,0:T(8,128)(2,1)} %get-tuple-element.129), channel_id=1, source_target_pairs={{0,32},{16,48},{32,0},{48,16},{64,96},{80,112},{96,64},{112,80},{1... | collective-permute-start | bytes 98312 | tf_op jit(solution)/shard_map/ppermute | solution.py:25
  221.4 10.3 %collective-permute-start.13 = (bf16[64,256]{1,0:T(8,128)(2,1)S(1)}, bf16[64,256]{1,0:T(8,128)(2,1)S(1)}, u32[]{:S(2)}, u32[]{:S(2)}) collective-permute-start(bf16[64,256]{1,0:T(8,128)(2,1)S(1)} %broadcast_select_fusion.3), channel_id=1, source_target_pairs={{0,16},{16,0},{32,48},{48,32},{64,80},{80,64},{96,112},{112,96},{1... | collective-permute-start | bytes 98312 | tf_op jit(solution)/shard_map/ppermute | solution.py:25
  234.3 5.4 %all-to-all-start.8 = ((bf16[8,64,256]{2,1,0:T(8,128)(2,1)}), bf16[8,64,256]{2,1,0:T(8,128)(2,1)}, u32[]{:S(2)}, u32[]{:S(2)}) async-start(bf16[8,64,256]{2,1,0:T(8,128)(2,1)} %broadcast_in_dim.55), calls=%async_computation.8 | async-start | bytes 524288 | tf_op jit(solution)/shard_map/all_to_all | solution.py:15
  239.7 8.7 %all-to-all-done.8 = bf16[8,64,256]{2,1,0:T(8,128)(2,1)} async-done(((bf16[8,64,256]{2,1,0:T(8,128)(2,1)}), bf16[8,64,256]{2,1,0:T(8,128)(2,1)}, u32[]{:S(2)}, u32[]{:S(2)}) %all-to-all-start.8) | async-done | bytes 262176 | tf_op jit(solution)/shard_map/all_to_all | solution.py:15
  254.6 5.2 %all-to-all-start.9 = ((bf16[8,64,256]{2,1,0:T(8,128)(2,1)}), bf16[8,64,256]{2,1,0:T(8,128)(2,1)S(1)}, u32[]{:S(2)}, u32[]{:S(2)}) async-start(bf16[8,64,256]{2,1,0:T(8,128)(2,1)} %broadcast_in_dim.56), calls=%async_computation.9 | async-start | bytes 524288 | tf_op jit(solution)/shard_map/all_to_all | solution.py:15
  261.1 7.8 %all-to-all-done.9 = bf16[8,64,256]{2,1,0:T(8,128)(2,1)S(1)} async-done(((bf16[8,64,256]{2,1,0:T(8,128)(2,1)}), bf16[8,64,256]{2,1,0:T(8,128)(2,1)S(1)}, u32[]{:S(2)}, u32[]{:S(2)}) %all-to-all-start.9) | async-done | bytes 262176 | tf_op jit(solution)/shard_map/all_to_all | solution.py:15
  275.9 4.8 %all-to-all-start.10 = ((bf16[8,64,256]{2,1,0:T(8,128)(2,1)}), bf16[8,64,256]{2,1,0:T(8,128)(2,1)S(1)}, u32[]{:S(2)}, u32[]{:S(2)}) async-start(bf16[8,64,256]{2,1,0:T(8,128)(2,1)} %broadcast_in_dim.57), calls=%async_computation.10 | async-start | bytes 524288 | tf_op jit(solution)/shard_map/all_to_all | solution.py:15
  283.4 6.3 %all-to-all-done.10 = bf16[8,64,256]{2,1,0:T(8,128)(2,1)S(1)} async-done(((bf16[8,64,256]{2,1,0:T(8,128)(2,1)}), bf16[8,64,256]{2,1,0:T(8,128)(2,1)S(1)}, u32[]{:S(2)}, u32[]{:S(2)}) %all-to-all-start.10) | async-done | bytes 262176 | tf_op jit(solution)/shard_map/all_to_all | solution.py:15
  293.7 4.8 %all-to-all-start.11 = ((bf16[8,64,256]{2,1,0:T(8,128)(2,1)}), bf16[8,64,256]{2,1,0:T(8,128)(2,1)S(1)}, u32[]{:S(2)}, u32[]{:S(2)}) async-start(bf16[8,64,256]{2,1,0:T(8,128)(2,1)} %broadcast_in_dim.107), calls=%async_computation.11 | async-start | bytes 524288 | tf_op jit(solution)/shard_map/all_to_all | solution.py:15
  298.5 9.0 %all-to-all-done.11 = bf16[8,64,256]{2,1,0:T(8,128)(2,1)S(1)} async-done(((bf16[8,64,256]{2,1,0:T(8,128)(2,1)}), bf16[8,64,256]{2,1,0:T(8,128)(2,1)S(1)}, u32[]{:S(2)}, u32[]{:S(2)}) %all-to-all-start.11) | async-done | bytes 262176 | tf_op jit(solution)/shard_map/all_to_all | solution.py:15
  (128 shorter events, 105.3 us)
Async XLA Ops:
  2.8 6.8 %all-to-all-start.1 = ((bf16[2,2,2048,128]{3,2,1,0:T(8,128)(2,1)}), bf16[2,2,2048,128]{3,2,1,0:T(8,128)(2,1)S(1)}, u32[]{:S(2)}, u32[]{:S(2)}) async-start(bf16[2,2,2048,128]{3,2,1,0:T(8,128)(2,1)} %broadcast_in_dim.47), calls=%async_computation.1 | async-start | bytes 4194304 | tf_op jit(solution)/shard_map/all_to_all | solution.py:15
  10.3 20.1 %all-to-all-start = ((bf16[8,64,256]{2,1,0:T(8,128)(2,1)}), bf16[8,64,256]{2,1,0:T(8,128)(2,1)S(1)}, u32[]{:S(2)}, u32[]{:S(2)}) async-start(bf16[8,64,256]{2,1,0:T(8,128)(2,1)} %broadcast_in_dim.46), calls=%async_computation | async-start | bytes 524288 | tf_op jit(solution)/shard_map/all_to_all | solution.py:15
  30.4 42.2 %copy-start.6 = (s32[2,16]{1,0:T(2,128)S(1)}, s32[2,16]{1,0:T(2,128)}, u32[]{:S(2)}) copy-start(s32[2,16]{1,0:T(2,128)} %param.25) | copy-start | bytes 388
  30.5 11.0 %collective-permute-start = (bf16[64,256]{1,0:T(8,128)(2,1)S(1)}, bf16[64,256]{1,0:T(8,128)(2,1)S(1)}, u32[]{:S(2)}, u32[]{:S(2)}) collective-permute-start(bf16[64,256]{1,0:T(8,128)(2,1)S(1)} %select_convert_fusion), channel_id=1, source_target_pairs={{0,256},{16,272},{32,288},{48,304},{64,320},{80,336},{96,352},{112... | collective-permute-start | bytes 98312 | tf_op jit(solution)/shard_map/ppermute | solution.py:25
  41.5 6.7 %collective-permute-start.1 = (bf16[64,256]{1,0:T(8,128)(2,1)S(1)}, bf16[64,256]{1,0:T(8,128)(2,1)S(1)}, u32[]{:S(2)}, u32[]{:S(2)}) collective-permute-start(bf16[64,256]{1,0:T(8,128)(2,1)S(1)} %broadcast_select_fusion.7), channel_id=1, source_target_pairs={{0,128},{16,144},{32,160},{48,176},{64,192},{80,208},{96,224},{112... | collective-permute-start | bytes 98312 | tf_op jit(solution)/shard_map/ppermute | solution.py:25
  48.2 5.8 %collective-permute-start.2 = (bf16[64,256]{1,0:T(8,128)(2,1)S(1)}, bf16[64,256]{1,0:T(8,128)(2,1)S(1)}, u32[]{:S(2)}, u32[]{:S(2)}) collective-permute-start(bf16[64,256]{1,0:T(8,128)(2,1)S(1)} %broadcast_select_fusion.8), channel_id=1, source_target_pairs={{0,64},{16,80},{32,96},{48,112},{64,0},{80,16},{96,32},{112,48},{1... | collective-permute-start | bytes 98312 | tf_op jit(solution)/shard_map/ppermute | solution.py:25
  54.0 7.4 %collective-permute-start.3 = (bf16[64,256]{1,0:T(8,128)(2,1)S(1)}, bf16[64,256]{1,0:T(8,128)(2,1)S(1)}, u32[]{:S(2)}, u32[]{:S(2)}) collective-permute-start(bf16[64,256]{1,0:T(8,128)(2,1)S(1)} %broadcast_select_fusion.10), channel_id=1, source_target_pairs={{0,32},{16,48},{32,0},{48,16},{64,96},{80,112},{96,64},{112,80},{1... | collective-permute-start | bytes 98312 | tf_op jit(solution)/shard_map/ppermute | solution.py:25
  61.4 5.8 %collective-permute-start.4 = (bf16[64,256]{1,0:T(8,128)(2,1)S(1)}, bf16[64,256]{1,0:T(8,128)(2,1)S(1)}, u32[]{:S(2)}, u32[]{:S(2)}) collective-permute-start(bf16[64,256]{1,0:T(8,128)(2,1)S(1)} %broadcast_select_fusion.13), channel_id=1, source_target_pairs={{0,16},{16,0},{32,48},{48,32},{64,80},{80,64},{96,112},{112,96},{1... | collective-permute-start | bytes 98312 | tf_op jit(solution)/shard_map/ppermute | solution.py:25
  67.9 13.7 %all-to-all-start.2 = ((bf16[8,64,256]{2,1,0:T(8,128)(2,1)}), bf16[8,64,256]{2,1,0:T(8,128)(2,1)S(1)}, u32[]{:S(2)}, u32[]{:S(2)}) async-start(bf16[8,64,256]{2,1,0:T(8,128)(2,1)} %broadcast_in_dim.48), calls=%async_computation.2 | async-start | bytes 524288 | tf_op jit(solution)/shard_map/all_to_all | solution.py:15
  82.4 13.8 %all-to-all-start.3 = ((bf16[8,64,256]{2,1,0:T(8,128)(2,1)}), bf16[8,64,256]{2,1,0:T(8,128)(2,1)S(1)}, u32[]{:S(2)}, u32[]{:S(2)}) async-start(bf16[8,64,256]{2,1,0:T(8,128)(2,1)} %broadcast_in_dim.49), calls=%async_computation.3 | async-start | bytes 524288 | tf_op jit(solution)/shard_map/all_to_all | solution.py:15
  96.8 6.7 %collective-permute-start.5 = (bf16[64,256]{1,0:T(8,128)(2,1)S(1)}, bf16[64,256]{1,0:T(8,128)(2,1)S(1)}, u32[]{:S(2)}, u32[]{:S(2)}) collective-permute-start(bf16[64,256]{1,0:T(8,128)(2,1)S(1)} %get-tuple-element.131), channel_id=1, source_target_pairs={{0,128},{16,144},{32,160},{48,176},{64,192},{80,208},{96,224},{112... | collective-permute-start | bytes 98312 | tf_op jit(solution)/shard_map/ppermute | solution.py:25
  103.5 5.8 %collective-permute-start.6 = (bf16[64,256]{1,0:T(8,128)(2,1)S(1)}, bf16[64,256]{1,0:T(8,128)(2,1)S(1)}, u32[]{:S(2)}, u32[]{:S(2)}) collective-permute-start(bf16[64,256]{1,0:T(8,128)(2,1)S(1)} %broadcast_select_fusion.6), channel_id=1, source_target_pairs={{0,64},{16,80},{32,96},{48,112},{64,0},{80,16},{96,32},{112,48},{1... | collective-permute-start | bytes 98312 | tf_op jit(solution)/shard_map/ppermute | solution.py:25
  109.4 7.3 %collective-permute-start.7 = (bf16[64,256]{1,0:T(8,128)(2,1)S(1)}, bf16[64,256]{1,0:T(8,128)(2,1)S(1)}, u32[]{:S(2)}, u32[]{:S(2)}) collective-permute-start(bf16[64,256]{1,0:T(8,128)(2,1)S(1)} %broadcast_select_fusion.9), channel_id=1, source_target_pairs={{0,32},{16,48},{32,0},{48,16},{64,96},{80,112},{96,64},{112,80},{1... | collective-permute-start | bytes 98312 | tf_op jit(solution)/shard_map/ppermute | solution.py:25
  116.7 5.8 %collective-permute-start.8 = (bf16[64,256]{1,0:T(8,128)(2,1)S(1)}, bf16[64,256]{1,0:T(8,128)(2,1)S(1)}, u32[]{:S(2)}, u32[]{:S(2)}) collective-permute-start(bf16[64,256]{1,0:T(8,128)(2,1)S(1)} %broadcast_select_fusion.12), channel_id=1, source_target_pairs={{0,16},{16,0},{32,48},{48,32},{64,80},{80,64},{96,112},{112,96},{1... | collective-permute-start | bytes 98312 | tf_op jit(solution)/shard_map/ppermute | solution.py:25
  123.2 14.0 %all-to-all-start.4 = ((bf16[8,64,256]{2,1,0:T(8,128)(2,1)}), bf16[8,64,256]{2,1,0:T(8,128)(2,1)S(1)}, u32[]{:S(2)}, u32[]{:S(2)}) async-start(bf16[8,64,256]{2,1,0:T(8,128)(2,1)} %broadcast_in_dim.50), calls=%async_computation.4 | async-start | bytes 524288 | tf_op jit(solution)/shard_map/all_to_all | solution.py:15
  140.3 14.6 %all-to-all-start.5 = ((bf16[8,64,256]{2,1,0:T(8,128)(2,1)}), bf16[8,64,256]{2,1,0:T(8,128)(2,1)S(1)}, u32[]{:S(2)}, u32[]{:S(2)}) async-start(bf16[8,64,256]{2,1,0:T(8,128)(2,1)} %broadcast_in_dim.51), calls=%async_computation.5 | async-start | bytes 524288 | tf_op jit(solution)/shard_map/all_to_all | solution.py:15
  154.9 22.7 %copy-start.5 = (f32[64,256]{1,0:T(8,128)}, f32[64,256]{1,0:T(8,128)S(1)}, u32[]{:S(2)}) copy-start(f32[64,256]{1,0:T(8,128)S(1)} %get-tuple-element.143) | copy-start | bytes 196612
  155.8 5.8 %collective-permute-start.9 = (bf16[64,256]{1,0:T(8,128)(2,1)S(1)}, bf16[64,256]{1,0:T(8,128)(2,1)S(1)}, u32[]{:S(2)}, u32[]{:S(2)}) collective-permute-start(bf16[64,256]{1,0:T(8,128)(2,1)S(1)} %fusion.20), channel_id=1, source_target_pairs={{0,64},{16,80},{32,96},{48,112},{64,0},{80,16},{96,32},{112,48},{1... | collective-permute-start | bytes 98312 | tf_op jit(solution)/shard_map/ppermute | solution.py:25
  161.6 7.8 %collective-permute-start.10 = (bf16[64,256]{1,0:T(8,128)(2,1)S(1)}, bf16[64,256]{1,0:T(8,128)(2,1)S(1)}, u32[]{:S(2)}, u32[]{:S(2)}) collective-permute-start(bf16[64,256]{1,0:T(8,128)(2,1)S(1)} %broadcast_select_fusion.5), channel_id=1, source_target_pairs={{0,32},{16,48},{32,0},{48,16},{64,96},{80,112},{96,64},{112,80},{1... | collective-permute-start | bytes 98312 | tf_op jit(solution)/shard_map/ppermute | solution.py:25
  169.4 7.4 %collective-permute-start.11 = (bf16[64,256]{1,0:T(8,128)(2,1)S(1)}, bf16[64,256]{1,0:T(8,128)(2,1)S(1)}, u32[]{:S(2)}, u32[]{:S(2)}) collective-permute-start(bf16[64,256]{1,0:T(8,128)(2,1)S(1)} %broadcast_select_fusion.11), channel_id=1, source_target_pairs={{0,16},{16,0},{32,48},{48,32},{64,80},{80,64},{96,112},{112,96},{1... | collective-permute-start | bytes 98312 | tf_op jit(solution)/shard_map/ppermute | solution.py:25
  177.6 14.6 %all-to-all-start.6 = ((bf16[8,64,256]{2,1,0:T(8,128)(2,1)}), bf16[8,64,256]{2,1,0:T(8,128)(2,1)S(1)}, u32[]{:S(2)}, u32[]{:S(2)}) async-start(bf16[8,64,256]{2,1,0:T(8,128)(2,1)} %broadcast_in_dim.52), calls=%async_computation.6 | async-start | bytes 524288 | tf_op jit(solution)/shard_map/all_to_all | solution.py:15
  196.0 14.5 %all-to-all-start.7 = ((bf16[8,64,256]{2,1,0:T(8,128)(2,1)}), bf16[8,64,256]{2,1,0:T(8,128)(2,1)}, u32[]{:S(2)}, u32[]{:S(2)}) async-start(bf16[8,64,256]{2,1,0:T(8,128)(2,1)} %broadcast_in_dim.54), calls=%async_computation.7 | async-start | bytes 524288 | tf_op jit(solution)/shard_map/all_to_all | solution.py:15
  212.7 7.9 %collective-permute-start.12 = (bf16[64,256]{1,0:T(8,128)(2,1)}, bf16[64,256]{1,0:T(8,128)(2,1)}, u32[]{:S(2)}, u32[]{:S(2)}) collective-permute-start(bf16[64,256]{1,0:T(8,128)(2,1)} %get-tuple-element.129), channel_id=1, source_target_pairs={{0,32},{16,48},{32,0},{48,16},{64,96},{80,112},{96,64},{112,80},{1... | collective-permute-start | bytes 98312 | tf_op jit(solution)/shard_map/ppermute | solution.py:25
  221.4 12.2 %collective-permute-start.13 = (bf16[64,256]{1,0:T(8,128)(2,1)S(1)}, bf16[64,256]{1,0:T(8,128)(2,1)S(1)}, u32[]{:S(2)}, u32[]{:S(2)}) collective-permute-start(bf16[64,256]{1,0:T(8,128)(2,1)S(1)} %broadcast_select_fusion.3), channel_id=1, source_target_pairs={{0,16},{16,0},{32,48},{48,32},{64,80},{80,64},{96,112},{112,96},{1... | collective-permute-start | bytes 98312 | tf_op jit(solution)/shard_map/ppermute | solution.py:25
  234.3 14.1 %all-to-all-start.8 = ((bf16[8,64,256]{2,1,0:T(8,128)(2,1)}), bf16[8,64,256]{2,1,0:T(8,128)(2,1)}, u32[]{:S(2)}, u32[]{:S(2)}) async-start(bf16[8,64,256]{2,1,0:T(8,128)(2,1)} %broadcast_in_dim.55), calls=%async_computation.8 | async-start | bytes 524288 | tf_op jit(solution)/shard_map/all_to_all | solution.py:15
  254.6 14.2 %all-to-all-start.9 = ((bf16[8,64,256]{2,1,0:T(8,128)(2,1)}), bf16[8,64,256]{2,1,0:T(8,128)(2,1)S(1)}, u32[]{:S(2)}, u32[]{:S(2)}) async-start(bf16[8,64,256]{2,1,0:T(8,128)(2,1)} %broadcast_in_dim.56), calls=%async_computation.9 | async-start | bytes 524288 | tf_op jit(solution)/shard_map/all_to_all | solution.py:15
  260.8 8.5 %copy-start.4 = (f32[64,256]{1,0:T(8,128)S(1)}, f32[64,256]{1,0:T(8,128)}, u32[]{:S(2)}) copy-start(f32[64,256]{1,0:T(8,128)} %get-tuple-element.130) | copy-start | bytes 196612
  269.4 5.8 %collective-permute-start.14 = (bf16[64,256]{1,0:T(8,128)(2,1)S(1)}, bf16[64,256]{1,0:T(8,128)(2,1)S(1)}, u32[]{:S(2)}, u32[]{:S(2)}) collective-permute-start(bf16[64,256]{1,0:T(8,128)(2,1)S(1)} %fusion.22), channel_id=1, source_target_pairs={{0,16},{16,0},{32,48},{48,32},{64,80},{80,64},{96,112},{112,96},{1... | collective-permute-start | bytes 98312 | tf_op jit(solution)/shard_map/ppermute | solution.py:25
  275.9 13.8 %all-to-all-start.10 = ((bf16[8,64,256]{2,1,0:T(8,128)(2,1)}), bf16[8,64,256]{2,1,0:T(8,128)(2,1)S(1)}, u32[]{:S(2)}, u32[]{:S(2)}) async-start(bf16[8,64,256]{2,1,0:T(8,128)(2,1)} %broadcast_in_dim.57), calls=%async_computation.10 | async-start | bytes 524288 | tf_op jit(solution)/shard_map/all_to_all | solution.py:15
  282.5 10.1 %copy-start.1 = (bf16[1,16,128,256]{3,2,1,0:T(8,128)(2,1)S(1)}, bf16[1,16,128,256]{3,2,1,0:T(8,128)(2,1)}, u32[]{:S(2)}) copy-start(bf16[1,16,128,256]{3,2,1,0:T(8,128)(2,1)} %get-tuple-element.135) | copy-start | bytes 3145732
  292.6 14.9 %copy-start = (bf16[1,2048,2,128]{1,3,2,0:T(8,128)(2,1)S(1)}, bf16[1,2048,2,128]{1,3,2,0:T(8,128)(2,1)}, u32[]{:S(2)}) copy-start(bf16[1,2048,2,128]{1,3,2,0:T(8,128)(2,1)} %get-tuple-element.133) | copy-start | bytes 3145732
  293.7 13.8 %all-to-all-start.11 = ((bf16[8,64,256]{2,1,0:T(8,128)(2,1)}), bf16[8,64,256]{2,1,0:T(8,128)(2,1)S(1)}, u32[]{:S(2)}, u32[]{:S(2)}) async-start(bf16[8,64,256]{2,1,0:T(8,128)(2,1)} %broadcast_in_dim.107), calls=%async_computation.11 | async-start | bytes 524288 | tf_op jit(solution)/shard_map/all_to_all | solution.py:15
  (2 other events, 4.7 us)
where the time goes:
time: 311 us; the launch traced here: 309 us
  starting transfers between devices  138 us (44%)
  waiting for transfers between devices  126 us (41%)
  local copies, waits for them, and re-layouts  33.7 us (11%)
  other arithmetic  9.14 us (3%)
    all_to_all x12, waiting for transfers between devices, from_everyone(): lax.all_to_all(jnp.broadcast_to(x[None], (peers, *x.shape)), axis, 0, 0,...  92.8 us
    ppermute x15, starting transfers between devices, swapped(): return lax.ppermute(value, axis, pairs)  75.3 us
    all_to_all x12, starting transfers between devices, from_everyone(): lax.all_to_all(jnp.broadcast_to(x[None], (peers, *x.shape)), axis, 0, 0,...  62.9 us
    ppermute x15, waiting for transfers between devices, swapped(): return lax.ppermute(value, axis, pairs)  32.8 us
    broadcast_in_dim x13, local copies, waits for them, and re-layouts, from_everyone(): jnp.broadcast_to(x[None], (peers, *x.shape))  10.7 us
  transfers between devices with their start and end apart: 27, of which 27 were waited for; matrix products, arithmetic and copies ran while one was open for 4% of the time, Pallas kernels for 0%

commit v1 on v0

v1 whole, which is shorter than its diff:
```python
import jax
import jax.numpy as jnp
from jax import lax
from jax.experimental import pallas as pl
from jax.experimental.pallas import tpu as pltpu
from jax.sharding import PartitionSpec as P

MESH = pl.DeviceIdType.MESH
BF16 = jnp.bfloat16
F32 = jnp.float32
RING = 8
FAR_FIRST = (4, 3, 5, 2, 6, 1, 7, 0)


def device(leaf, row, core):
    return {"leaf": leaf, "rows": row, "rhs": core}


def remote(source, target, sent, arrived, where):
    return pltpu.make_async_remote_copy(
        source, target, sent, arrived, device_id=where, device_id_type=MESH
    )


def kernel(
    block_rows, right_side, inverse_diag, lower_blocks, out,
    rhs, inv, low, anc_up, anc_lo, red, piece, result,
    load_sem, half_send, half_recv, red_send, red_recv, piece_send, piece_recv,
    pass_send, pass_recv, out_sem,
):
    leaf = lax.axis_index("leaf")
    row = lax.axis_index("rows")
    core = lax.axis_index("rhs")
    has_upper = leaf < 31
    even = leaf % 2 == 0
    trail = jnp.int32(0)
    for power in range(1, 5):
        trail = trail + ((leaf + 1) % 2**power == 0).astype(jnp.int32)
    depth = 4 - trail
    span = jnp.where(trail == 0, 1, jnp.where(trail == 1, 2, jnp.where(trail == 2, 4, jnp.where(trail == 3, 8, 16))))
    parent = jnp.where((leaf // (2 * span)) % 2 == 0, leaf + span, leaf - span)
    child_a = leaf - span // 2
    child_b = leaf + span // 2
    below_root = jnp.logical_and(has_upper, depth >= 1)
    splits = jnp.logical_and(has_upper, depth <= 3)
    sibling = jnp.where(even, leaf + 1, leaf - 1)

    loads = []
    for slot in (1, 0):
        loads.append(pltpu.make_async_copy(right_side.at[slot], rhs.at[slot], load_sem.at[slot, 0]))
        own = inv.at[slot, :, pl.ds(pl.multiple_of(core * 128, 128), 128)]
        loads.append(pltpu.make_async_copy(inverse_diag.at[slot], own, load_sem.at[slot, 1]))
        loads.append(pltpu.make_async_copy(lower_blocks.at[slot], low.at[slot], load_sem.at[slot, 2]))
    for copy in loads:
        copy.start()

    barrier = pltpu.get_barrier_semaphore()

    def greet(where):
        pl.semaphore_signal(barrier, inc=1, device_id=where, device_id_type=MESH)

    for step in range(1, RING):
        greet(device(leaf, (row + step) % RING, core))
    greet(device(leaf, row, 1 - core))
    for step in range(RING):
        greet(device(sibling, (row + step) % RING, core))

    @pl.when(below_root)
    def _():
        for step in range(RING):
            greet(device(parent, (row + step) % RING, core))

    @pl.when(splits)
    def _():
        for step in range(RING):
            greet(device(child_a, (row + step) % RING, core))
            greet(device(child_b, (row + step) % RING, core))

    pl.semaphore_wait(
        barrier,
        16 + 8 * below_root.astype(jnp.int32) + 16 * splits.astype(jnp.int32),
    )

    halves = []
    for slot in (1, 0):
        there = inv.at[slot, :, pl.ds(pl.multiple_of(core * 128, 128), 128)]
        copy = remote(
            inverse_diag.at[slot], there, half_send.at[slot], half_recv.at[slot],
            device(leaf, row, 1 - core),
        )
        copy.start()
        halves.append(copy)

    def offset_of(slot, ancestors, limit):
        picked = jnp.concatenate(
            [ancestors[jnp.clip(block_rows[slot, r], 0, limit)] for r in range(16)], axis=1
        )
        return jnp.dot(picked, low[slot].reshape(2048, 256), preferred_element_type=F32)

    def reduce_and_solve(slot, reduced):
        mine = pl.ds(2 * row, 2)
        rounded = reduced.astype(BF16)
        red[slot, 2 * row] = rounded[:, :128]
        red[slot, 2 * row + 1] = rounded[:, 128:]
        copies = []
        for step in FAR_FIRST[:-1]:
            copy = remote(
                red.at[slot, mine], red.at[slot, mine],
                red_send.at[slot, step], red_recv.at[slot, step],
                device(leaf, (row + step) % RING, core),
            )
            copy.start()
            copies.append(copy)
        for copy in copies:
            copy.wait_recv()
        full = jnp.concatenate([red[slot, b] for b in range(16)], axis=1)
        return jnp.dot(full, inv[slot], preferred_element_type=F32)

    def finish_sends(slot):
        for step in range(1, RING):
            remote(
                red.at[slot, pl.ds(2 * row, 2)], red.at[slot, pl.ds(2 * row, 2)],
                red_send.at[slot, step], red_recv.at[slot, step],
                device(leaf, (row + step) % RING, core),
            ).wait_send()

    def hand_on(level, child, which):
        level_blocks = pl.ds(16 * level, 16)
        return remote(
            anc_up.at[level_blocks], anc_up.at[level_blocks],
            pass_send.at[level, which], pass_recv.at[level],
            device(child, row, core),
        )

    def hand_across(level):
        level_blocks = pl.ds(16 * level, 16)
        return remote(
            anc_up.at[level_blocks], anc_lo.at[level_blocks],
            pass_send.at[level, 2], pass_recv.at[level + 4],
            device(sibling, row, core),
        )

    def piece_copy(child, step, which, ancestors, group):
        return remote(
            piece, ancestors.at[pl.ds(16 * depth + 2 * row, 2)],
            piece_send.at[which, step], piece_recv.at[group, step],
            device(child, (row + step) % RING, core),
        )

    crosses_all = leaf % 4 == 2

    for level in range(3):
        @pl.when(jnp.logical_and(below_root, level < depth - 1))
        def _():
            hand_on(level, parent, 0).wait_recv()

            @pl.when(splits)
            def _():
                hand_on(level, child_a, 0).start()
                hand_on(level, child_b, 1).start()

            @pl.when(crosses_all)
            def _():
                hand_across(level).start()

    loads[0].wait()
    loads[1].wait()
    loads[2].wait()
    halves[0].wait_recv()

    @pl.when(below_root)
    def _():
        for step in FAR_FIRST:
            remote(
                piece, anc_up.at[pl.ds(0, 2)], piece_send.at[0, step], piece_recv.at[0, step],
                device(parent, row, core),
            ).wait_recv()

    @pl.when(has_upper)
    def _():
        @pl.when(below_root)
        def _():
            rhs[1] = rhs[1] - offset_of(1, anc_up, 63)

        solved = reduce_and_solve(1, rhs[1])
        result[1] = solved
        rounded = solved.astype(BF16)
        piece[0] = rounded[:, :128]
        piece[1] = rounded[:, 128:]

        @pl.when(splits)
        def _():
            for step in FAR_FIRST:
                piece_copy(child_a, step, 0, anc_up, 0).start()
                piece_copy(child_b, step, 1, anc_up, 0).start()

            for level in range(3):
                @pl.when(level == depth - 1)
                def _():
                    hand_on(level, child_a, 0).start()
                    hand_on(level, child_b, 1).start()

        @pl.when(even)
        def _():
            for step in FAR_FIRST:
                piece_copy(sibling, step, 1, anc_lo, 1).start()
                if step:
                    piece_copy(leaf, step, 0, anc_lo, 1).start()
            anc_lo[64 + 2 * row] = rounded[:, :128]
            anc_lo[64 + 2 * row + 1] = rounded[:, 128:]
            hand_across(3).start()
            for block in range(64):
                anc_lo[block] = anc_up[block]

    @pl.when(leaf == 31)
    def _():
        result[1] = jnp.zeros_like(result[1])

    upper_out = pltpu.make_async_copy(result.at[1], out.at[1], out_sem.at[1])
    upper_out.start()

    loads[3].wait()
    loads[4].wait()
    loads[5].wait()
    halves[1].wait_recv()

    @pl.when(leaf % 4 == 1)
    def _():
        for block in range(48):
            anc_lo[block] = anc_up[block]

    @pl.when(leaf % 4 == 3)
    def _():
        for level in range(3):
            hand_across(level).wait_recv()

    @pl.when(jnp.logical_not(even))
    def _():
        hand_across(3).wait_recv()
        remote(
            piece, anc_lo.at[pl.ds(0, 2)], piece_send.at[0, 0], piece_recv.at[1, 0],
            device(sibling, row, core),
        ).wait_recv()

    for step in FAR_FIRST[:-1]:
        remote(
            piece, anc_lo.at[pl.ds(0, 2)], piece_send.at[0, step], piece_recv.at[1, step],
            device(sibling, row, core),
        ).wait_recv()

    solved_lower = reduce_and_solve(0, rhs[0] - offset_of(0, anc_lo, 79))
    result[0] = solved_lower
    lower_out = pltpu.make_async_copy(result.at[0], out.at[0], out_sem.at[0])
    lower_out.start()

    for copy in halves:
        copy.wait_send()
    finish_sends(0)

    @pl.when(has_upper)
    def _():
        finish_sends(1)

        @pl.when(splits)
        def _():
            for step in range(RING):
                piece_copy(child_a, step, 0, anc_up, 0).wait_send()
                piece_copy(child_b, step, 1, anc_up, 0).wait_send()
            for level in range(3):
                @pl.when(level < depth)
                def _():
                    hand_on(level, child_a, 0).wait_send()
                    hand_on(level, child_b, 1).wait_send()

        @pl.when(even)
        def _():
            for step in range(RING):
                piece_copy(sibling, step, 1, anc_lo, 1).wait_send()
                if step:
                    piece_copy(leaf, step, 0, anc_lo, 1).wait_send()
            hand_across(3).wait_send()

        @pl.when(crosses_all)
        def _():
            for level in range(3):
                hand_across(level).wait_send()

    upper_out.wait()
    lower_out.wait()


def local(right_side, inverse_diag, lower_blocks, block_rows):
    anywhere = pl.BlockSpec(memory_space=pl.ANY)
    dma = pltpu.SemaphoreType.DMA
    return pl.pallas_call(
        kernel,
        name="sweep",
        out_shape=jax.ShapeDtypeStruct((2, 64, 256), F32),
        in_specs=[pl.BlockSpec(memory_space=pltpu.SMEM), anywhere, anywhere, anywhere],
        out_specs=anywhere,
        scratch_shapes=[
            pltpu.VMEM((2, 64, 256), F32),
            pltpu.VMEM((2, 2048, 256), BF16),
            pltpu.VMEM((2, 16, 128, 256), BF16),
            pltpu.VMEM((64, 64, 128), BF16),
            pltpu.VMEM((80, 64, 128), BF16),
            pltpu.VMEM((2, 16, 64, 128), BF16),
            pltpu.VMEM((2, 64, 128), BF16),
            pltpu.VMEM((2, 64, 256), F32),
            dma((2, 3)),
            dma((2,)),
            dma((2,)),
            dma((2, 8)),
            dma((2, 8)),
            dma((2, 8)),
            dma((2, 8)),
            dma((4, 3)),
            dma((8,)),
            dma((2,)),
        ],
        compiler_params=pltpu.CompilerParams(
            collective_id=0, has_side_effects=True, vmem_limit_bytes=56 * 2**20
        ),
    )(block_rows, right_side, inverse_diag, lower_blocks)


def solution(mesh):
    return jax.shard_map(
        local,
        mesh=mesh,
        in_specs=(
            P("leaf", "rhs", "rows"),
            P("leaf", None, ("rows", "rhs")),
            P("leaf", None, None, "rows"),
            P("leaf", None),
        ),
        out_specs=P("leaf", "rhs", "rows"),
        check_vma=False,
    )
```

time: 311 us -> 137 us (0.44)
  the two profiles are of different devices: /device:TPU:8 before, /device:TPU:5 now
where the time goes in v1:
time: 137 us; the launch traced here: 136 us
  Pallas kernels  135 us (99%)
  local copies, waits for them, and re-layouts  1.57 us (1%)
    pallas_call x1, Pallas kernels, local(): pl.pallas_call(kernel, name='sweep', out_shape=jax.ShapeDtypeStruct((2, 6...  135 us

profile of v1, /device:TPU:5, one launch (start us, length us, event | category | flops | bytes accessed | tf_op | source)
XLA Modules:
  0.0 136.5 jit_solution(5072560505497103271)
XLA Ops:
  0.0 134.9 %sweep.1 = f32[2,64,256]{2,1,0:T(8,128)} custom-call(s32[2,16]{1,0:T(2,128)} %block_rows.1, f32[2,64,256]{2,1,0:T(8,128)} %right_side.1, bf16[2,2048,128]{2,1,0:T(8,128)(2,1)} %inverse_diag.1, bf16[2,16,128,256]{3,2,1,0:T(8,128)(2,1)} %lower_blocks.1), custom_call_target="tpu_custom_call" | custom-call | tf_op jit(solution)/shard_map/sweep/pallas_call | solution.py:295
  134.9 1.6 %copy.6 = f32[2,64,256]{2,1,0:T(8,128)} copy(f32[2,64,256]{2,1,0:T(8,128)} %sweep.1) | data formatting | bytes 262144

commit v2 on v0

v2 whole, which is shorter than its diff:
```python
import jax
import jax.numpy as jnp
from jax import lax
from jax.experimental import pallas as pl
from jax.experimental.pallas import tpu as pltpu
from jax.sharding import PartitionSpec as P

MESH = pl.DeviceIdType.MESH
BF16 = jnp.bfloat16
F32 = jnp.float32
RING = 8
LEVELS = 5
CHUNKS = 2
ROWS = 32
FAR_FIRST = (4, 3, 5, 2, 6, 1, 7)


def device(leaf, row, core):
    return {"leaf": leaf, "rows": row, "rhs": core}


def remote(source, target, sent, arrived, where):
    return pltpu.make_async_remote_copy(
        source, target, sent, arrived, device_id=where, device_id_type=MESH
    )


def depth_of(leaf):
    trail = jnp.int32(0)
    for power in range(1, 6):
        trail = trail + ((leaf + 1) % 2**power == 0).astype(jnp.int32)
    return 4 - trail


def kernel(
    block_rows, right_side, inverse_diag, lower_blocks, out,
    rhs, inv, low, anc_0, anc_1, red, result,
    load_sem, half_send, half_recv, red_send, red_recv, hop_send, hop_recv,
    ring_send, ring_recv, out_sem,
):
    anc = (anc_0, anc_1)
    leaf = lax.axis_index("leaf")
    row = lax.axis_index("rows")
    core = lax.axis_index("rhs")
    even = leaf % 2 == 0
    depth = depth_of(leaf)
    half_span = jnp.int32(0)
    for level in range(4):
        half_span = half_span + jnp.where(depth == level, 2 ** (3 - level), 0)
    span = jnp.maximum(2 * half_span, 1)
    parent = jnp.where((leaf // (2 * span)) % 2 == 0, leaf + span, leaf - span)
    child_a = leaf - half_span
    child_b = leaf + half_span
    has_upper = depth >= 0
    below_root = depth >= 1
    splits = jnp.logical_and(has_upper, depth <= 3)
    sibling = jnp.where(even, leaf + 1, leaf - 1)
    sibling_depth = depth_of(sibling)
    mine_cols = pl.ds(pl.multiple_of(core * 128, 128), 128)

    loads = {}
    for slot in (1, 0):
        loads[slot, 0] = pltpu.make_async_copy(right_side.at[slot], rhs.at[slot], load_sem.at[slot, 0])
        loads[slot, 1] = pltpu.make_async_copy(
            inverse_diag.at[slot], inv.at[slot, :, mine_cols], load_sem.at[slot, 1]
        )
        loads[slot, 2] = pltpu.make_async_copy(lower_blocks.at[slot], low.at[slot], load_sem.at[slot, 2])
    for copy in loads.values():
        copy.start()

    barrier = pltpu.get_barrier_semaphore()

    def greet(where):
        pl.semaphore_signal(barrier, inc=1, device_id=where, device_id_type=MESH)

    for step in FAR_FIRST:
        greet(device(leaf, (row + step) % RING, core))
    greet(device(leaf, row, 1 - core))
    greet(device(sibling, row, core))

    @pl.when(below_root)
    def _():
        greet(device(parent, row, core))

    @pl.when(splits)
    def _():
        greet(device(child_a, row, core))
        greet(device(child_b, row, core))

    pl.semaphore_wait(
        barrier, 9 + below_root.astype(jnp.int32) + 2 * splits.astype(jnp.int32)
    )

    halves = {
        slot: remote(
            inverse_diag.at[slot], inv.at[slot, :, mine_cols], half_send.at[slot], half_recv.at[slot],
            device(leaf, row, 1 - core),
        )
        for slot in (1, 0)
    }

    def ring_copies(level, chunk):
        piece = anc[chunk].at[pl.ds(16 * level + 2 * row, 2)]
        return [
            remote(
                piece, piece, ring_send.at[level, chunk, step], ring_recv.at[level, chunk, step],
                device(leaf, (row + step) % RING, core),
            )
            for step in FAR_FIRST
        ]

    def red_copies(slot, chunk):
        piece = red.at[slot, chunk, pl.ds(2 * row, 2)]
        return [
            remote(
                piece, piece, red_send.at[slot, chunk, step], red_recv.at[slot, chunk, step],
                device(leaf, (row + step) % RING, core),
            )
            for step in FAR_FIRST
        ]

    def hop(level, chunk, where, which):
        piece = anc[chunk].at[pl.ds(16 * level + 2 * row, 2)]
        return remote(
            piece, piece, hop_send.at[level, chunk, which], hop_recv.at[level, chunk],
            device(where, row, core),
        )

    def each_hop(level, chunk, act):
        @pl.when(jnp.logical_and(splits, depth >= level))
        def _():
            act(hop(level, chunk, child_a, 0))
            act(hop(level, chunk, child_b, 1))

        @pl.when(jnp.logical_and(even, sibling_depth < level))
        def _():
            act(hop(level, chunk, sibling, 0))

    def start(copy):
        copy.start()

    def spread(level, chunk):
        each_hop(level, chunk, start)
        for copy in ring_copies(level, chunk):
            copy.start()

    def wait_ring(level, chunk):
        for copy in ring_copies(level, chunk):
            copy.wait_recv()

    def set_reduced(slot, chunk, offset):
        span_rows = pl.ds(ROWS * chunk, ROWS)
        value = rhs[slot, span_rows]
        if offset is not None:
            value = value - offset
        rounded = value.astype(BF16)
        red[slot, chunk, 2 * row] = rounded[:, :128]
        red[slot, chunk, 2 * row + 1] = rounded[:, 128:]
        for copy in red_copies(slot, chunk):
            copy.start()

    def offset_of(slot, chunk, limit):
        picked = jnp.concatenate(
            [anc[chunk][jnp.clip(block_rows[slot, r], 0, limit)] for r in range(16)], axis=1
        )
        return jnp.dot(picked, low[slot].reshape(2048, 256), preferred_element_type=F32)

    def solve(slot, chunk):
        for copy in red_copies(slot, chunk):
            copy.wait_recv()
        full = jnp.concatenate([red[slot, chunk, b] for b in range(16)], axis=1)
        solved = jnp.dot(full, inv[slot], preferred_element_type=F32)
        result[slot, pl.ds(ROWS * chunk, ROWS)] = solved
        return solved

    def wait_weights(slot):
        loads[slot, 1].wait()
        halves[slot].wait_recv()

    loads[1, 0].wait()

    for level in range(LEVELS):
        @pl.when(depth != level)
        def _():
            if level == 0:
                halves[1].start()
                halves[0].start()
            for chunk in range(CHUNKS):
                hop(level, chunk, leaf, 0).wait_recv()
                spread(level, chunk)

        @pl.when(depth == level)
        def _():
            if level > 0:
                loads[1, 2].wait()
            for chunk in range(CHUNKS):
                for above in range(level):
                    wait_ring(above, chunk)
                set_reduced(1, chunk, offset_of(1, chunk, 16 * level - 1) if level else None)
            if level == 0:
                halves[1].start()
                halves[0].start()
            wait_weights(1)
            for chunk in range(CHUNKS):
                rounded = solve(1, chunk).astype(BF16)
                anc[chunk][16 * level + 2 * row] = rounded[:, :128]
                anc[chunk][16 * level + 2 * row + 1] = rounded[:, 128:]
                spread(level, chunk)
            if level == 0:
                loads[1, 2].wait()

    @pl.when(depth < 0)
    def _():
        wait_weights(1)
        loads[1, 2].wait()
        result[1] = jnp.zeros_like(result[1])

    upper_out = pltpu.make_async_copy(result.at[1], out.at[1], out_sem.at[1])
    upper_out.start()

    loads[0, 0].wait()
    loads[0, 2].wait()
    wait_weights(0)
    for chunk in range(CHUNKS):
        for level in range(LEVELS):
            @pl.when(depth <= level)
            def _():
                wait_ring(level, chunk)

        set_reduced(0, chunk, offset_of(0, chunk, 79))
    for chunk in range(CHUNKS):
        solve(0, chunk)
    lower_out = pltpu.make_async_copy(result.at[0], out.at[0], out_sem.at[0])
    lower_out.start()

    halves[1].wait_send()
    halves[0].wait_send()

    def wait_send(copy):
        copy.wait_send()

    for chunk in range(CHUNKS):
        for level in range(LEVELS):
            each_hop(level, chunk, wait_send)
            for copy in ring_copies(level, chunk):
                copy.wait_send()
        for copy in red_copies(0, chunk):
            copy.wait_send()

        @pl.when(has_upper)
        def _():
            for copy in red_copies(1, chunk):
                copy.wait_send()

    upper_out.wait()
    lower_out.wait()


def local(right_side, inverse_diag, lower_blocks, block_rows):
    anywhere = pl.BlockSpec(memory_space=pl.ANY)
    dma = pltpu.SemaphoreType.DMA
    return pl.pallas_call(
        kernel,
        name="sweep",
        out_shape=jax.ShapeDtypeStruct((2, 64, 256), F32),
        in_specs=[pl.BlockSpec(memory_space=pltpu.SMEM), anywhere, anywhere, anywhere],
        out_specs=anywhere,
        scratch_shapes=[
            pltpu.VMEM((2, 64, 256), F32),
            pltpu.VMEM((2, 2048, 256), BF16),
            pltpu.VMEM((2, 16, 128, 256), BF16),
            pltpu.VMEM((80, ROWS, 128), BF16),
            pltpu.VMEM((80, ROWS, 128), BF16),
            pltpu.VMEM((2, CHUNKS, 16, ROWS, 128), BF16),
            pltpu.VMEM((2, 64, 256), F32),
            dma((2, 3)),
            dma((2,)),
            dma((2,)),
            dma((2, CHUNKS, 8)),
            dma((2, CHUNKS, 8)),
            dma((LEVELS, CHUNKS, 2)),
            dma((LEVELS, CHUNKS)),
            dma((LEVELS, CHUNKS, 8)),
            dma((LEVELS, CHUNKS, 8)),
            dma((2,)),
        ],
        compiler_params=pltpu.CompilerParams(
            collective_id=0, has_side_effects=True, vmem_limit_bytes=56 * 2**20
        ),
    )(block_rows, right_side, inverse_diag, lower_blocks)


def solution(mesh):
    return jax.shard_map(
        local,
        mesh=mesh,
        in_specs=(
            P("leaf", "rhs", "rows"),
            P("leaf", None, ("rows", "rhs")),
            P("leaf", None, None, "rows"),
            P("leaf", None),
        ),
        out_specs=P("leaf", "rhs", "rows"),
        check_vma=False,
    )
```

time: 311 us -> 99.4 us (0.32)
  the two profiles are of different devices: /device:TPU:8 before, /device:TPU:2 now
where the time goes in v2:
time: 99.4 us; the launch traced here: 99.3 us
  Pallas kernels  97.7 us (98%)
  local copies, waits for them, and re-layouts  1.57 us (2%)
    pallas_call x1, Pallas kernels, local(): pl.pallas_call(kernel, name='sweep', out_shape=jax.ShapeDtypeStruct((2, 6...  97.7 us

profile of v2, /device:TPU:2, one launch (start us, length us, event | category | flops | bytes accessed | tf_op | source)
XLA Modules:
  0.0 99.3 jit_solution(13563613430534286555)
XLA Ops:
  0.0 97.7 %sweep.1 = f32[2,64,256]{2,1,0:T(8,128)} custom-call(s32[2,16]{1,0:T(2,128)} %block_rows.1, f32[2,64,256]{2,1,0:T(8,128)} %right_side.1, bf16[2,2048,128]{2,1,0:T(8,128)(2,1)} %inverse_diag.1, bf16[2,16,128,256]{3,2,1,0:T(8,128)(2,1)} %lower_blocks.1), custom_call_target="tpu_custom_call" | custom-call | tf_op jit(solution)/shard_map/sweep/pallas_call | solution.py:262
  97.7 1.6 %copy.6 = f32[2,64,256]{2,1,0:T(8,128)} copy(f32[2,64,256]{2,1,0:T(8,128)} %sweep.1) | data formatting | bytes 262144

commit v3 on v2

--- a/solution.py
+++ b/solution.py
@@ -33,10 +33,10 @@
 
 
 def kernel(
-    block_rows, right_side, inverse_diag, lower_blocks, out,
-    rhs, inv, low, anc_0, anc_1, red, result,
+    block_rows_in, right_side, inverse_diag, lower_blocks, out,
+    block_rows, rhs, inv, low, anc_0, anc_1, red, result,
     load_sem, half_send, half_recv, red_send, red_recv, hop_send, hop_recv,
-    ring_send, ring_recv, out_sem,
+    ring_send, ring_recv, direct_send, out_sem, rows_sem, ready,
 ):
     anc = (anc_0, anc_1)
     leaf = lax.axis_index("leaf")
@@ -58,6 +58,35 @@
     sibling_depth = depth_of(sibling)
     mine_cols = pl.ds(pl.multiple_of(core * 128, 128), 128)
 
+    barrier = pltpu.get_barrier_semaphore()
+
+    def greet(where):
+        pl.semaphore_signal(barrier, inc=1, device_id=where, device_id_type=MESH)
+
+    def report(where):
+        pl.semaphore_signal(ready, inc=1, device_id=where, device_id_type=MESH)
+
+    for step in FAR_FIRST:
+        greet(device(leaf, (row + step) % RING, core))
+    greet(device(leaf, row, 1 - core))
+
+    @pl.when(depth == 3)
+    def _():
+        for step in range(RING):
+            greet(device(child_a, (row + step) % RING, core))
+            greet(device(child_b, (row + step) % RING, core))
+
+    @pl.when(jnp.logical_and(has_upper, depth <= 2))
+    def _():
+        greet(device(child_a, row, core))
+        greet(device(child_b, row, core))
+
+    @pl.when(even)
+    def _():
+        for step in range(RING):
+            greet(device(sibling, (row + step) % RING, core))
+
+    block_rows_copy = pltpu.make_async_copy(block_rows_in, block_rows, rows_sem.at[0])
     loads = {}
     for slot in (1, 0):
         loads[slot, 0] = pltpu.make_async_copy(right_side.at[slot], rhs.at[slot], load_sem.at[slot, 0])
@@ -67,29 +96,29 @@
         loads[slot, 2] = pltpu.make_async_copy(lower_blocks.at[slot], low.at[slot], load_sem.at[slot, 2])
     for copy in loads.values():
         copy.start()
-
-    barrier = pltpu.get_barrier_semaphore()
-
-    def greet(where):
-        pl.semaphore_signal(barrier, inc=1, device_id=where, device_id_type=MESH)
-
-    for step in FAR_FIRST:
-        greet(device(leaf, (row + step) % RING, core))
-    greet(device(leaf, row, 1 - core))
-    greet(device(sibling, row, core))
-
-    @pl.when(below_root)
-    def _():
-        greet(device(parent, row, core))
-
-    @pl.when(splits)
-    def _():
-        greet(device(child_a, row, core))
-        greet(device(child_b, row, core))
-
-    pl.semaphore_wait(
-        barrier, 9 + below_root.astype(jnp.int32) + 2 * splits.astype(jnp.int32)
-    )
+    block_rows_copy.start()
+
+    from_parent = jnp.where(depth == 4, 8, jnp.where(below_root, 1, 0))
+    pl.semaphore_wait(barrier, 8 + from_parent + jnp.where(even, 0, 8))
+
+    @pl.when(depth == 4)
+    def _():
+        for step in range(RING):
+            report(device(parent, (row + step) % RING, core))
+
+    @pl.when(jnp.logical_and(below_root, depth <= 3))
+    def _():
+        report(device(parent, row, core))
+
+    @pl.when(jnp.logical_not(even))
+    def _():
+        for step in range(RING):
+            report(device(sibling, (row + step) % RING, core))
+
+    def wait_ready():
+        @pl.when(has_upper)
+        def _():
+            pl.semaphore_wait(ready, jnp.where(even, 8, jnp.where(depth == 3, 16, 2)))
 
     halves = {
         slot: remote(
@@ -126,23 +155,62 @@
             device(where, row, core),
         )
 
+    def direct(chunk, where, which, step):
+        level = jnp.maximum(depth, 0)
+        piece = anc[chunk].at[pl.ds(16 * level + 2 * row, 2)]
+        arrived = ring_recv.at[level, chunk, step] if step else hop_recv.at[level, chunk]
+        return remote(
+            piece, piece, direct_send.at[chunk, which, step], arrived,
+            device(where, (row + step) % RING, core),
+        )
+
     def each_hop(level, chunk, act):
-        @pl.when(jnp.logical_and(splits, depth >= level))
+        @pl.when(jnp.logical_and(splits, jnp.logical_and(depth >= level, jnp.logical_or(depth > level, depth < 3))))
         def _():
             act(hop(level, chunk, child_a, 0))
             act(hop(level, chunk, child_b, 1))
 
-        @pl.when(jnp.logical_and(even, sibling_depth < level))
-        def _():
-            act(hop(level, chunk, sibling, 0))
+        if level < 4:
+            @pl.when(jnp.logical_and(even, sibling_depth < level))
+            def _():
+                act(hop(level, chunk, sibling, 0))
+
+        if level == 3:
+            @pl.when(depth == 3)
+            def _():
+                for step in (*FAR_FIRST, 0):
+                    act(direct(chunk, child_a, 0, step))
+                    act(direct(chunk, child_b, 1, step))
+
+        if level == 4:
+            @pl.when(even)
+            def _():
+                for step in (*FAR_FIRST, 0):
+                    act(direct(chunk, sibling, 0, step))
+
+    def gathers(level):
+        if level == 3:
+            return depth != 4
+        if level == 4:
+            return even
+        return depth < 9
 
     def start(copy):
         copy.start()
 
+    def each_ring(level, chunk, act):
+        if level < 3:
+            for copy in ring_copies(level, chunk):
+                act(copy)
+        else:
+            @pl.when(gathers(level))
+            def _():
+                for copy in ring_copies(level, chunk):
+                    act(copy)
+
     def spread(level, chunk):
         each_hop(level, chunk, start)
-        for copy in ring_copies(level, chunk):
-            copy.start()
+        each_ring(level, chunk, start)
 
     def wait_ring(level, chunk):
         for copy in ring_copies(level, chunk):
@@ -179,12 +247,17 @@
 
     loads[1, 0].wait()
 
+    @pl.when(depth != 0)
+    def _():
+        block_rows_copy.wait()
+
     for level in range(LEVELS):
         @pl.when(depth != level)
         def _():
             if level == 0:
                 halves[1].start()
                 halves[0].start()
+                wait_ready()
             for chunk in range(CHUNKS):
                 hop(level, chunk, leaf, 0).wait_recv()
                 spread(level, chunk)
@@ -199,15 +272,18 @@
                 set_reduced(1, chunk, offset_of(1, chunk, 16 * level - 1) if level else None)
             if level == 0:
                 halves[1].start()
-                halves[0].start()
             wait_weights(1)
             for chunk in range(CHUNKS):
                 rounded = solve(1, chunk).astype(BF16)
                 anc[chunk][16 * level + 2 * row] = rounded[:, :128]
                 anc[chunk][16 * level + 2 * row + 1] = rounded[:, 128:]
+                if level == 0 and chunk == 0:
+                    wait_ready()
                 spread(level, chunk)
             if level == 0:
+                halves[0].start()
                 loads[1, 2].wait()
+                block_rows_copy.wait()
 
     @pl.when(depth < 0)
     def _():
@@ -242,8 +318,7 @@
     for chunk in range(CHUNKS):
         for level in range(LEVELS):
             each_hop(level, chunk, wait_send)
-            for copy in ring_copies(level, chunk):
-                copy.wait_send()
+            each_ring(level, chunk, wait_send)
         for copy in red_copies(0, chunk):
             copy.wait_send()
 
@@ -263,9 +338,10 @@
         kernel,
         name="sweep",
         out_shape=jax.ShapeDtypeStruct((2, 64, 256), F32),
-        in_specs=[pl.BlockSpec(memory_space=pltpu.SMEM), anywhere, anywhere, anywhere],
+        in_specs=[anywhere] * 4,
         out_specs=anywhere,
         scratch_shapes=[
+            pltpu.SMEM((2, 16), jnp.int32),
             pltpu.VMEM((2, 64, 256), F32),
             pltpu.VMEM((2, 2048, 256), BF16),
             pltpu.VMEM((2, 16, 128, 256), BF16),
@@ -282,7 +358,10 @@
             dma((LEVELS, CHUNKS)),
             dma((LEVELS, CHUNKS, 8)),
             dma((LEVELS, CHUNKS, 8)),
+            dma((CHUNKS, 2, 8)),
             dma((2,)),
+            dma((1,)),
+            pltpu.SemaphoreType.REGULAR,
         ],
         compiler_params=pltpu.CompilerParams(
             collective_id=0, has_side_effects=True, vmem_limit_bytes=56 * 2**20

time: 99.4 us -> 101 us (1.016)
  the two profiles are of different devices: /device:TPU:2 before, /device:TPU:64 now
where the time goes in v3:
time: 101 us; the launch traced here: 100 us
  Pallas kernels  98.9 us (98%)
  local copies, waits for them, and re-layouts  1.57 us (2%)
    pallas_call x1, Pallas kernels, local(): pl.pallas_call(kernel, name='sweep', out_shape=jax.ShapeDtypeStruct((2, 6...  98.9 us

profile of v3, /device:TPU:64, one launch (start us, length us, event | category | flops | bytes accessed | tf_op | source)
XLA Modules:
  0.0 100.5 jit_solution(4853822708305390066)
XLA Ops:
  0.0 98.9 %sweep.1 = f32[2,64,256]{2,1,0:T(8,128)} custom-call(s32[2,16]{1,0:T(2,128)} %block_rows_in.1, f32[2,64,256]{2,1,0:T(8,128)} %right_side.1, bf16[2,2048,128]{2,1,0:T(8,128)(2,1)} %inverse_diag.1, bf16[2,16,128,256]{3,2,1,0:T(8,128)(2,1)} %lower_blocks.1), custom_call_target="tpu_custom_call" | custom-call | tf_op jit(solution)/shard_map/sweep/pallas_call | solution.py:337
  98.9 1.6 %copy.6 = f32[2,64,256]{2,1,0:T(8,128)} copy(f32[2,64,256]{2,1,0:T(8,128)} %sweep.1) | data formatting | bytes 262144

commit v4 on v3

--- a/solution.py
+++ b/solution.py
@@ -10,9 +10,12 @@
 F32 = jnp.float32
 RING = 8
 LEVELS = 5
-CHUNKS = 2
-ROWS = 32
+CHUNKS = 4
+ROWS = 16
 FAR_FIRST = (4, 3, 5, 2, 6, 1, 7)
+FAR_UPPER = ()
+FAR_LAST = ()
+FAR_SIBLING = ()
 
 
 def device(leaf, row, core):
@@ -33,12 +36,12 @@
 
 
 def kernel(
-    block_rows_in, right_side, inverse_diag, lower_blocks, out,
-    block_rows, rhs, inv, low, anc_0, anc_1, red, result,
+    block_rows_in, right_side, inverse_diag, lower_blocks, result,
+    block_rows, rhs, inv, low, anc_0, anc_1, anc_2, anc_3, red,
     load_sem, half_send, half_recv, red_send, red_recv, hop_send, hop_recv,
-    ring_send, ring_recv, direct_send, out_sem, rows_sem, ready,
+    ring_send, ring_recv, rows_sem, ready,
 ):
-    anc = (anc_0, anc_1)
+    anc = (anc_0, anc_1, anc_2, anc_3,)
     leaf = lax.axis_index("leaf")
     row = lax.axis_index("rows")
     core = lax.axis_index("rhs")
@@ -70,20 +73,16 @@
         greet(device(leaf, (row + step) % RING, core))
     greet(device(leaf, row, 1 - core))
 
-    @pl.when(depth == 3)
-    def _():
-        for step in range(RING):
-            greet(device(child_a, (row + step) % RING, core))
-            greet(device(child_b, (row + step) % RING, core))
-
-    @pl.when(jnp.logical_and(has_upper, depth <= 2))
-    def _():
-        greet(device(child_a, row, core))
-        greet(device(child_b, row, core))
+    for is_last, far in ((True, FAR_LAST), (False, FAR_UPPER)):
+        @pl.when(depth == 3 if is_last else jnp.logical_and(has_upper, depth <= 2))
+        def _():
+            for step in (*far, 0):
+                greet(device(child_a, (row + step) % RING, core))
+                greet(device(child_b, (row + step) % RING, core))
 
     @pl.when(even)
     def _():
-        for step in range(RING):
+        for step in (*FAR_SIBLING, 0):
             greet(device(sibling, (row + step) % RING, core))
 
     block_rows_copy = pltpu.make_async_copy(block_rows_in, block_rows, rows_sem.at[0])
@@ -98,27 +97,28 @@
         copy.start()
     block_rows_copy.start()
 
-    from_parent = jnp.where(depth == 4, 8, jnp.where(below_root, 1, 0))
-    pl.semaphore_wait(barrier, 8 + from_parent + jnp.where(even, 0, 8))
-
-    @pl.when(depth == 4)
-    def _():
-        for step in range(RING):
-            report(device(parent, (row + step) % RING, core))
-
-    @pl.when(jnp.logical_and(below_root, depth <= 3))
-    def _():
-        report(device(parent, row, core))
+    upper_hops, last_hops, sibling_hops = 1 + len(FAR_UPPER), 1 + len(FAR_LAST), 1 + len(FAR_SIBLING)
+    from_parent = jnp.where(depth == 4, last_hops, jnp.where(below_root, upper_hops, 0))
+    pl.semaphore_wait(barrier, 8 + from_parent + jnp.where(even, 0, sibling_hops))
+
+    for is_last, far in ((True, FAR_LAST), (False, FAR_UPPER)):
+        @pl.when(depth == 4 if is_last else jnp.logical_and(below_root, depth <= 3))
+        def _():
+            for step in (*far, 0):
+                report(device(parent, (row + step) % RING, core))
 
     @pl.when(jnp.logical_not(even))
     def _():
-        for step in range(RING):
+        for step in (*FAR_SIBLING, 0):
             report(device(sibling, (row + step) % RING, core))
 
     def wait_ready():
         @pl.when(has_upper)
         def _():
-            pl.semaphore_wait(ready, jnp.where(even, 8, jnp.where(depth == 3, 16, 2)))
+            pl.semaphore_wait(
+                ready,
+                jnp.where(even, sibling_hops, jnp.where(depth == 3, 2 * last_hops, 2 * upper_hops)),
+            )
 
     halves = {
         slot: remote(
@@ -128,7 +128,7 @@
         for slot in (1, 0)
     }
 
-    def ring_copies(level, chunk):
+    def ring_copies(level, chunk, skipped=()):
         piece = anc[chunk].at[pl.ds(16 * level + 2 * row, 2)]
         return [
             remote(
@@ -136,6 +136,7 @@
                 device(leaf, (row + step) % RING, core),
             )
             for step in FAR_FIRST
+            if step not in skipped
         ]
 
     def red_copies(slot, chunk):
@@ -148,65 +149,59 @@
             for step in FAR_FIRST
         ]
 
-    def hop(level, chunk, where, which):
-        piece = anc[chunk].at[pl.ds(16 * level + 2 * row, 2)]
-        return remote(
-            piece, piece, hop_send.at[level, chunk, which], hop_recv.at[level, chunk],
-            device(where, row, core),
-        )
-
-    def direct(chunk, where, which, step):
-        level = jnp.maximum(depth, 0)
+    def hop(level, chunk, where, which, step=0):
         piece = anc[chunk].at[pl.ds(16 * level + 2 * row, 2)]
         arrived = ring_recv.at[level, chunk, step] if step else hop_recv.at[level, chunk]
         return remote(
-            piece, piece, direct_send.at[chunk, which, step], arrived,
+            piece, piece, hop_send.at[level, chunk, which, step], arrived,
             device(where, (row + step) % RING, core),
         )
 
     def each_hop(level, chunk, act):
-        @pl.when(jnp.logical_and(splits, jnp.logical_and(depth >= level, jnp.logical_or(depth > level, depth < 3))))
-        def _():
-            act(hop(level, chunk, child_a, 0))
-            act(hop(level, chunk, child_b, 1))
-
-        if level < 4:
-            @pl.when(jnp.logical_and(even, sibling_depth < level))
+        for is_last, far in ((True, FAR_LAST), (False, FAR_UPPER)):
+            if level > (3 if is_last else 2):
+                continue
+
+            @pl.when(depth == 3 if is_last else jnp.logical_and(depth >= level, depth <= 2))
             def _():
-                act(hop(level, chunk, sibling, 0))
-
-        if level == 3:
-            @pl.when(depth == 3)
-            def _():
-                for step in (*FAR_FIRST, 0):
-                    act(direct(chunk, child_a, 0, step))
-                    act(direct(chunk, child_b, 1, step))
-
-        if level == 4:
-            @pl.when(even)
-            def _():
-                for step in (*FAR_FIRST, 0):
-                    act(direct(chunk, sibling, 0, step))
-
-    def gathers(level):
-        if level == 3:
-            return depth != 4
-        if level == 4:
-            return even
-        return depth < 9
+                for step in (0, *far):
+                    act(hop(level, chunk, child_a, 0, step))
+                    act(hop(level, chunk, child_b, 1, step))
+
+        @pl.when(jnp.logical_and(even, sibling_depth < level))
+        def _():
+            for step in (0, *FAR_SIBLING):
+                act(hop(level, chunk, sibling, 0, step))
 
     def start(copy):
         copy.start()
 
     def each_ring(level, chunk, act):
+        def run(skipped):
+            for copy in ring_copies(level, chunk, skipped):
+                act(copy)
+
+        if not (FAR_UPPER or FAR_LAST or FAR_SIBLING):
+            run(())
+            return
+
+        @pl.when(depth == level)
+        def _():
+            run(())
+
+        @pl.when(depth < level)
+        def _():
+            run(FAR_SIBLING)
+
+        if level < 4:
+            @pl.when(depth == 4)
+            def _():
+                run(FAR_LAST)
+
         if level < 3:
-            for copy in ring_copies(level, chunk):
-                act(copy)
-        else:
-            @pl.when(gathers(level))
+            @pl.when(jnp.logical_and(depth > level, depth < 4))
             def _():
-                for copy in ring_copies(level, chunk):
-                    act(copy)
+                run(FAR_UPPER)
 
     def spread(level, chunk):
         each_hop(level, chunk, start)
@@ -291,9 +286,6 @@
         loads[1, 2].wait()
         result[1] = jnp.zeros_like(result[1])
 
-    upper_out = pltpu.make_async_copy(result.at[1], out.at[1], out_sem.at[1])
-    upper_out.start()
-
     loads[0, 0].wait()
     loads[0, 2].wait()
     wait_weights(0)
@@ -306,8 +298,6 @@
         set_reduced(0, chunk, offset_of(0, chunk, 79))
     for chunk in range(CHUNKS):
         solve(0, chunk)
-    lower_out = pltpu.make_async_copy(result.at[0], out.at[0], out_sem.at[0])
-    lower_out.start()
 
     halves[1].wait_send()
     halves[0].wait_send()
@@ -327,9 +317,6 @@
             for copy in red_copies(1, chunk):
                 copy.wait_send()
 
-    upper_out.wait()
-    lower_out.wait()
-
 
 def local(right_side, inverse_diag, lower_blocks, block_rows):
     anywhere = pl.BlockSpec(memory_space=pl.ANY)
@@ -337,9 +324,9 @@
     return pl.pallas_call(
         kernel,
         name="sweep",
-        out_shape=jax.ShapeDtypeStruct((2, 64, 256), F32),
+        out_shape=pltpu.VMEM((2, 64, 256), F32),
         in_specs=[anywhere] * 4,
-        out_specs=anywhere,
+        out_specs=pl.BlockSpec(memory_space=pltpu.VMEM),
         scratch_shapes=[
             pltpu.SMEM((2, 16), jnp.int32),
             pltpu.VMEM((2, 64, 256), F32),
@@ -347,19 +334,18 @@
             pltpu.VMEM((2, 16, 128, 256), BF16),
             pltpu.VMEM((80, ROWS, 128), BF16),
             pltpu.VMEM((80, ROWS, 128), BF16),
+            pltpu.VMEM((80, ROWS, 128), BF16),
+            pltpu.VMEM((80, ROWS, 128), BF16),
             pltpu.VMEM((2, CHUNKS, 16, ROWS, 128), BF16),
-            pltpu.VMEM((2, 64, 256), F32),
             dma((2, 3)),
             dma((2,)),
             dma((2,)),
             dma((2, CHUNKS, 8)),
             dma((2, CHUNKS, 8)),
-            dma((LEVELS, CHUNKS, 2)),
+            dma((LEVELS, CHUNKS, 2, 8)),
             dma((LEVELS, CHUNKS)),
             dma((LEVELS, CHUNKS, 8)),
             dma((LEVELS, CHUNKS, 8)),
-            dma((CHUNKS, 2, 8)),
-            dma((2,)),
             dma((1,)),
             pltpu.SemaphoreType.REGULAR,
         ],

time: 101 us -> 96.5 us (0.955)
  the two profiles are of different devices: /device:TPU:64 before, /device:TPU:2 now
where the time goes in v4:
time: 96.5 us; the launch traced here: 96.4 us
  Pallas kernels  95.7 us (99%)
    pallas_call x1, Pallas kernels, local(): pl.pallas_call(kernel, name='sweep', out_shape=pltpu.VMEM((2, 64, 256), F...  95.7 us

profile of v4, /device:TPU:2, one launch (start us, length us, event | category | flops | bytes accessed | tf_op | source)
XLA Modules:
  0.0 96.4 jit_solution(2955217929634305537)
XLA Ops:
  0.0 95.7 %sweep.1 = f32[2,64,256]{2,1,0:T(8,128)S(1)} custom-call(s32[2,16]{1,0:T(2,128)} %block_rows_in.1, f32[2,64,256]{2,1,0:T(8,128)} %right_side.1, bf16[2,2048,128]{2,1,0:T(8,128)(2,1)} %inverse_diag.1, bf16[2,16,128,256]{3,2,1,0:T(8,128)(2,1)} %lower_blocks.1), custom_call_target="tpu_custom_call" | custom-call | tf_op jit(solution)/shard_map/sweep/pallas_call | solution.py:324
  95.7 0.7 copy.6

commit v5 on v4

--- a/solution.py
+++ b/solution.py
@@ -13,9 +13,7 @@
 CHUNKS = 4
 ROWS = 16
 FAR_FIRST = (4, 3, 5, 2, 6, 1, 7)
-FAR_UPPER = ()
-FAR_LAST = ()
-FAR_SIBLING = ()
+OTHERS = 2 * len(FAR_FIRST)
 
 
 def device(leaf, row, core):
@@ -73,17 +71,14 @@
         greet(device(leaf, (row + step) % RING, core))
     greet(device(leaf, row, 1 - core))
 
-    for is_last, far in ((True, FAR_LAST), (False, FAR_UPPER)):
-        @pl.when(depth == 3 if is_last else jnp.logical_and(has_upper, depth <= 2))
-        def _():
-            for step in (*far, 0):
-                greet(device(child_a, (row + step) % RING, core))
-                greet(device(child_b, (row + step) % RING, core))
+    @pl.when(splits)
+    def _():
+        greet(device(child_a, row, core))
+        greet(device(child_b, row, core))
 
     @pl.when(even)
     def _():
-        for step in (*FAR_SIBLING, 0):
-            greet(device(sibling, (row + step) % RING, core))
+        greet(device(sibling, row, core))
 
     block_rows_copy = pltpu.make_async_copy(block_rows_in, block_rows, rows_sem.at[0])
     loads = {}
@@ -97,28 +92,20 @@
         copy.start()
     block_rows_copy.start()
 
-    upper_hops, last_hops, sibling_hops = 1 + len(FAR_UPPER), 1 + len(FAR_LAST), 1 + len(FAR_SIBLING)
-    from_parent = jnp.where(depth == 4, last_hops, jnp.where(below_root, upper_hops, 0))
-    pl.semaphore_wait(barrier, 8 + from_parent + jnp.where(even, 0, sibling_hops))
-
-    for is_last, far in ((True, FAR_LAST), (False, FAR_UPPER)):
-        @pl.when(depth == 4 if is_last else jnp.logical_and(below_root, depth <= 3))
-        def _():
-            for step in (*far, 0):
-                report(device(parent, (row + step) % RING, core))
+    pl.semaphore_wait(barrier, 8 + below_root.astype(jnp.int32) + jnp.where(even, 0, 1))
+
+    @pl.when(below_root)
+    def _():
+        report(device(parent, row, core))
 
     @pl.when(jnp.logical_not(even))
     def _():
-        for step in (*FAR_SIBLING, 0):
-            report(device(sibling, (row + step) % RING, core))
+        report(device(sibling, row, core))
 
     def wait_ready():
         @pl.when(has_upper)
         def _():
-            pl.semaphore_wait(
-                ready,
-                jnp.where(even, sibling_hops, jnp.where(depth == 3, 2 * last_hops, 2 * upper_hops)),
-            )
+            pl.semaphore_wait(ready, jnp.where(even, 1, 2))
 
     halves = {
         slot: remote(
@@ -128,88 +115,58 @@
         for slot in (1, 0)
     }
 
-    def ring_copies(level, chunk, skipped=()):
+    def ring_copies(level, chunk):
         piece = anc[chunk].at[pl.ds(16 * level + 2 * row, 2)]
         return [
             remote(
-                piece, piece, ring_send.at[level, chunk, step], ring_recv.at[level, chunk, step],
+                piece, piece, ring_send.at[chunk], ring_recv.at[level, chunk],
                 device(leaf, (row + step) % RING, core),
             )
             for step in FAR_FIRST
-            if step not in skipped
         ]
 
     def red_copies(slot, chunk):
         piece = red.at[slot, chunk, pl.ds(2 * row, 2)]
         return [
             remote(
-                piece, piece, red_send.at[slot, chunk, step], red_recv.at[slot, chunk, step],
+                piece, piece, red_send.at[slot], red_recv.at[slot, chunk],
                 device(leaf, (row + step) % RING, core),
             )
             for step in FAR_FIRST
         ]
 
-    def hop(level, chunk, where, which, step=0):
+    def whole(chunk, blocks, sent, arrived):
+        part = anc[chunk].at[pl.ds(0, blocks)]
+        return remote(part, part, sent, arrived, device(leaf, row, 1 - core))
+
+    def wait_ring(level, chunk):
+        whole(chunk, OTHERS, ring_send.at[chunk], ring_recv.at[level, chunk]).wait_recv()
+
+    def wait_red(slot, chunk):
+        whole(chunk, OTHERS, red_send.at[slot], red_recv.at[slot, chunk]).wait_recv()
+
+    def hop(level, chunk, where, which):
         piece = anc[chunk].at[pl.ds(16 * level + 2 * row, 2)]
-        arrived = ring_recv.at[level, chunk, step] if step else hop_recv.at[level, chunk]
         return remote(
-            piece, piece, hop_send.at[level, chunk, which, step], arrived,
-            device(where, (row + step) % RING, core),
-        )
-
-    def each_hop(level, chunk, act):
-        for is_last, far in ((True, FAR_LAST), (False, FAR_UPPER)):
-            if level > (3 if is_last else 2):
-                continue
-
-            @pl.when(depth == 3 if is_last else jnp.logical_and(depth >= level, depth <= 2))
+            piece, piece, hop_send.at[level, which], hop_recv.at[level, chunk],
+            device(where, row, core),
+        )
+
+    def each_hop(level, act):
+        if level < 4:
+            @pl.when(jnp.logical_and(splits, depth >= level))
             def _():
-                for step in (0, *far):
-                    act(hop(level, chunk, child_a, 0, step))
-                    act(hop(level, chunk, child_b, 1, step))
+                act(child_a, 0)
+                act(child_b, 1)
 
         @pl.when(jnp.logical_and(even, sibling_depth < level))
         def _():
-            for step in (0, *FAR_SIBLING):
-                act(hop(level, chunk, sibling, 0, step))
-
-    def start(copy):
-        copy.start()
-
-    def each_ring(level, chunk, act):
-        def run(skipped):
-            for copy in ring_copies(level, chunk, skipped):
-                act(copy)
-
-        if not (FAR_UPPER or FAR_LAST or FAR_SIBLING):
-            run(())
-            return
-
-        @pl.when(depth == level)
-        def _():
-            run(())
-
-        @pl.when(depth < level)
-        def _():
-            run(FAR_SIBLING)
-
-        if level < 4:
-            @pl.when(depth == 4)
-            def _():
-                run(FAR_LAST)
-
-        if level < 3:
-            @pl.when(jnp.logical_and(depth > level, depth < 4))
-            def _():
-                run(FAR_UPPER)
+            act(sibling, 0)
 
     def spread(level, chunk):
-        each_hop(level, chunk, start)
-        each_ring(level, chunk, start)
-
-    def wait_ring(level, chunk):
+        each_hop(level, lambda where, which: hop(level, chunk, where, which).start())
         for copy in ring_copies(level, chunk):
-            copy.wait_recv()
+            copy.start()
 
     def set_reduced(slot, chunk, offset):
         span_rows = pl.ds(ROWS * chunk, ROWS)
@@ -229,8 +186,7 @@
         return jnp.dot(picked, low[slot].reshape(2048, 256), preferred_element_type=F32)
 
     def solve(slot, chunk):
-        for copy in red_copies(slot, chunk):
-            copy.wait_recv()
+        wait_red(slot, chunk)
         full = jnp.concatenate([red[slot, chunk, b] for b in range(16)], axis=1)
         solved = jnp.dot(full, inv[slot], preferred_element_type=F32)
         result[slot, pl.ds(ROWS * chunk, ROWS)] = solved
@@ -302,20 +258,20 @@
     halves[1].wait_send()
     halves[0].wait_send()
 
-    def wait_send(copy):
-        copy.wait_send()
-
+    for level in range(LEVELS):
+        each_hop(
+            level,
+            lambda where, which: whole(
+                0, 2 * CHUNKS, hop_send.at[level, which], hop_recv.at[level, 0]
+            ).wait_send(),
+        )
     for chunk in range(CHUNKS):
-        for level in range(LEVELS):
-            each_hop(level, chunk, wait_send)
-            each_ring(level, chunk, wait_send)
-        for copy in red_copies(0, chunk):
-            copy.wait_send()
-
-        @pl.when(has_upper)
-        def _():
-            for copy in red_copies(1, chunk):
-                copy.wait_send()
+        whole(chunk, LEVELS * OTHERS, ring_send.at[chunk], ring_recv.at[0, chunk]).wait_send()
+    whole(0, CHUNKS * OTHERS, red_send.at[0], red_recv.at[0, 0]).wait_send()
+
+    @pl.when(has_upper)
+    def _():
+        whole(0, CHUNKS * OTHERS, red_send.at[1], red_recv.at[1, 0]).wait_send()
 
 
 def local(right_side, inverse_diag, lower_blocks, block_rows):
@@ -340,12 +296,12 @@
             dma((2, 3)),
             dma((2,)),
             dma((2,)),
-            dma((2, CHUNKS, 8)),
-            dma((2, CHUNKS, 8)),
-            dma((LEVELS, CHUNKS, 2, 8)),
+            dma((2,)),
+            dma((2, CHUNKS)),
+            dma((LEVELS, 2)),
             dma((LEVELS, CHUNKS)),
-            dma((LEVELS, CHUNKS, 8)),
-            dma((LEVELS, CHUNKS, 8)),
+            dma((CHUNKS,)),
+            dma((LEVELS, CHUNKS)),
             dma((1,)),
             pltpu.SemaphoreType.REGULAR,
         ],

time: 96.5 us -> 88.9 us (0.921)
  Pallas kernels: 95.7 us -> 87.9 us
    pallas_call x1, Pallas kernels: 95.7 us -> 87.9 us  [local(): pl.pallas_call(kernel, name='sweep', out_shape=pltpu.VMEM((2, 64, 256), F...]
where the time goes in v5:
time: 88.9 us; the launch traced here: 88.6 us
  Pallas kernels  87.9 us (99%)
    pallas_call x1, Pallas kernels, local(): pl.pallas_call(kernel, name='sweep', out_shape=pltpu.VMEM((2, 64, 256), F...  87.9 us

profile of v5, /device:TPU:2, one launch (start us, length us, event | category | flops | bytes accessed | tf_op | source)
XLA Modules:
  0.0 88.6 jit_solution(11180080955074835697)
XLA Ops:
  0.0 87.9 %sweep.1 = f32[2,64,256]{2,1,0:T(8,128)S(1)} custom-call(s32[2,16]{1,0:T(2,128)} %block_rows_in.1, f32[2,64,256]{2,1,0:T(8,128)} %right_side.1, bf16[2,2048,128]{2,1,0:T(8,128)(2,1)} %inverse_diag.1, bf16[2,16,128,256]{3,2,1,0:T(8,128)(2,1)} %lower_blocks.1), custom_call_target="tpu_custom_call" | custom-call | tf_op jit(solution)/shard_map/sweep/pallas_call | solution.py:280
  88.0 0.7 copy.6

commit v6 on v5

--- a/solution.py
+++ b/solution.py
@@ -35,9 +35,9 @@
 
 def kernel(
     block_rows_in, right_side, inverse_diag, lower_blocks, result,
-    block_rows, rhs, inv, low, anc_0, anc_1, anc_2, anc_3, red,
+    block_rows, rhs, inv, low, anc_0, anc_1, anc_2, anc_3, last, red, full, fused, total,
     load_sem, half_send, half_recv, red_send, red_recv, hop_send, hop_recv,
-    ring_send, ring_recv, rows_sem, ready,
+    ring_send, ring_recv, rows_sem, pass_send, turn_send, turn_recv, across_send, across_recv, ready,
 ):
     anc = (anc_0, anc_1, anc_2, anc_3,)
     leaf = lax.axis_index("leaf")
@@ -115,8 +115,13 @@
         for slot in (1, 0)
     }
 
+    def piece_at(level, chunk):
+        if level == 4:
+            return last.at[chunk, pl.ds(2 * row, 2)]
+        return anc[chunk].at[pl.ds(16 * level + 2 * row, 2)]
+
     def ring_copies(level, chunk):
-        piece = anc[chunk].at[pl.ds(16 * level + 2 * row, 2)]
+        piece = piece_at(level, chunk)
         return [
             remote(
                 piece, piece, ring_send.at[chunk], ring_recv.at[level, chunk],
@@ -146,7 +151,7 @@
         whole(chunk, OTHERS, red_send.at[slot], red_recv.at[slot, chunk]).wait_recv()
 
     def hop(level, chunk, where, which):
-        piece = anc[chunk].at[pl.ds(16 * level + 2 * row, 2)]
+        piece = piece_at(level, chunk)
         return remote(
             piece, piece, hop_send.at[level, which], hop_recv.at[level, chunk],
             device(where, row, core),
@@ -154,7 +159,7 @@
 
     def each_hop(level, act):
         if level < 4:
-            @pl.when(jnp.logical_and(splits, depth >= level))
+            @pl.when(jnp.logical_and(depth >= level, depth <= (3 if level >= 2 else 2)))
             def _():
                 act(child_a, 0)
                 act(child_b, 1)
@@ -167,6 +172,83 @@
         each_hop(level, lambda where, which: hop(level, chunk, where, which).start())
         for copy in ring_copies(level, chunk):
             copy.start()
+
+    own_half = pl.ds(8 * core, 8)
+    quarters = (pl.ds(8 * core, 4), pl.ds(8 * core + 4, 4))
+
+    def turn(step, way, sub):
+        piece = (row + RING - way * (step - 1)) % RING
+        blocks = quarters[sub]
+        source = low.at[1, blocks] if step == 1 else full.at[piece, blocks]
+        side = 0 if way == 1 else 1
+        return remote(
+            source, full.at[piece, blocks], turn_send.at[side], turn_recv.at[step - 1, side, sub],
+            device(leaf, (row + RING + way) % RING, core),
+        )
+
+    def travels(step, side, sub):
+        return step < 4 or side == sub
+
+    def start_turn():
+        for sub in range(2):
+            for way in (1, -1):
+                turn(1, way, sub).start()
+
+    def pass_turn(step):
+        for sub in range(2):
+            for way, side in ((1, 0), (-1, 1)):
+                if not travels(step, side, sub):
+                    continue
+                piece = (row + RING - way * step) % RING
+                turn(step, way, sub).wait_recv()
+                if step < 4 and travels(step + 1, side, sub):
+                    turn(step + 1, way, sub).start()
+                blocks = full.at[piece, quarters[sub]]
+                remote(
+                    blocks, blocks, across_send.at[0], across_recv.at[step - 1],
+                    device(leaf, row, 1 - core),
+                ).start()
+
+    def fuse(step):
+        if step == 0:
+            own_low.wait()
+            pieces = [row]
+        elif step < 4:
+            pieces = [(row + step) % RING, (row + RING - step) % RING]
+        else:
+            pieces = [(row + step) % RING]
+        if step:
+            part = full.at[pl.ds(0, len(pieces)), own_half]
+            remote(
+                part, part, across_send.at[0], across_recv.at[step - 1], device(leaf, row, 1 - core)
+            ).wait_recv()
+
+        @pl.loop(0, 8)
+        def _(tile):
+            rows = pl.ds(pl.multiple_of(256 * tile, 256), 256)
+            product = None
+            for piece in pieces:
+                term = jnp.dot(
+                    full[piece, pl.ds(2 * tile, 2)].reshape(256, 256),
+                    inv[1, pl.ds(pl.multiple_of(256 * piece, 256), 256)],
+                    preferred_element_type=F32,
+                )
+                product = term if product is None else product + term
+            if step:
+                product = total[rows, :] + product
+            if step < 4:
+                total[rows, :] = product
+            else:
+                fused[rows, :] = product.astype(BF16)
+
+    own_low = pltpu.make_async_copy(lower_blocks.at[1], full.at[row], across_recv.at[4])
+
+    def pass_down(level, chunk, where):
+        blocks = anc[chunk].at[pl.ds(16 * level, 16)]
+        return remote(
+            blocks, blocks, pass_send.at[level], ring_recv.at[level, chunk],
+            device(where, row, core),
+        )
 
     def set_reduced(slot, chunk, offset):
         span_rows = pl.ds(ROWS * chunk, ROWS)
@@ -179,10 +261,13 @@
         for copy in red_copies(slot, chunk):
             copy.start()
 
+    def picked_of(slot, chunk, limit):
+        return jnp.concatenate(
+            [anc[chunk][jnp.clip(block_rows[slot, r], 0, limit)] for r in range(16)], axis=1
+        )
+
     def offset_of(slot, chunk, limit):
-        picked = jnp.concatenate(
-            [anc[chunk][jnp.clip(block_rows[slot, r], 0, limit)] for r in range(16)], axis=1
-        )
+        picked = picked_of(slot, chunk, limit)
         return jnp.dot(picked, low[slot].reshape(2048, 256), preferred_element_type=F32)
 
     def solve(slot, chunk):
@@ -202,23 +287,91 @@
     def _():
         block_rows_copy.wait()
 
+    @pl.when(depth == 4)
+    def _():
+        own_low.start()
+        halves[1].start()
+        for chunk in range(CHUNKS):
+            set_reduced(1, chunk, None)
+        loads[1, 2].wait()
+        start_turn()
+        halves[0].start()
+        wait_ready()
+
+    @pl.when(jnp.logical_and(depth != 0, depth != 4))
+    def _():
+        halves[1].start()
+        halves[0].start()
+        wait_ready()
+
     for level in range(LEVELS):
-        @pl.when(depth != level)
-        def _():
-            if level == 0:
-                halves[1].start()
-                halves[0].start()
-                wait_ready()
-            for chunk in range(CHUNKS):
-                hop(level, chunk, leaf, 0).wait_recv()
-                spread(level, chunk)
+        if level < 3:
+            @pl.when(depth == 4)
+            def _():
+                if level == 0:
+                    pass_turn(1)
+                    wait_weights(1)
+                    fuse(0)
+                    pass_turn(2)
+                    fuse(1)
+                elif level == 1:
+                    fuse(2)
+                    pass_turn(3)
+                else:
+                    fuse(3)
+                    pass_turn(4)
+                for chunk in range(CHUNKS):
+                    if level < 2:
+                        whole(chunk, 16, pass_send.at[level], ring_recv.at[level, chunk]).wait_recv()
+                        each_hop(level, lambda where, which: hop(level, chunk, where, which).start())
+                    else:
+                        hop(level, chunk, leaf, 0).wait_recv()
+                        spread(level, chunk)
+                if level == 2:
+                    fuse(4)
+                    for chunk in range(CHUNKS):
+                        solve(1, chunk)
+
+            @pl.when(jnp.logical_and(depth != level, depth != 4))
+            def _():
+                for chunk in range(CHUNKS):
+                    hop(level, chunk, leaf, 0).wait_recv()
+                    spread(level, chunk)
+
+                if level < 2:
+                    @pl.when(depth == 3)
+                    def _():
+                        for chunk in range(CHUNKS):
+                            wait_ring(level, chunk)
+                            pass_down(level, chunk, child_a).start()
+                            pass_down(level, chunk, child_b).start()
+        else:
+            @pl.when(depth != level)
+            def _():
+                for chunk in range(CHUNKS):
+                    hop(level, chunk, leaf, 0).wait_recv()
+                    spread(level, chunk)
 
         @pl.when(depth == level)
         def _():
+            if level == 4:
+                for chunk in range(CHUNKS):
+                    wait_ring(2, chunk)
+                    wait_ring(3, chunk)
+                    rows = pl.ds(ROWS * chunk, ROWS)
+                    solved = result[1, rows] - jnp.dot(
+                        picked_of(1, chunk, 63), fused[...], preferred_element_type=F32
+                    )
+                    result[1, rows] = solved
+                    rounded = solved.astype(BF16)
+                    last[chunk, 2 * row] = rounded[:, :128]
+                    last[chunk, 2 * row + 1] = rounded[:, 128:]
+                    spread(level, chunk)
+                return
             if level > 0:
                 loads[1, 2].wait()
             for chunk in range(CHUNKS):
-                for above in range(level):
+                for above in range(2 if level == 3 else 0, level):
                     wait_ring(above, chunk)
                 set_reduced(1, chunk, offset_of(1, chunk, 16 * level - 1) if level else None)
             if level == 0:
@@ -251,6 +404,8 @@
             def _():
                 wait_ring(level, chunk)
 
+        for block in range(16):
+            anc[chunk][64 + block] = last[chunk, block]
         set_reduced(0, chunk, offset_of(0, chunk, 79))
     for chunk in range(CHUNKS):
         solve(0, chunk)
@@ -266,7 +421,31 @@
             ).wait_send(),
         )
     for chunk in range(CHUNKS):
-        whole(chunk, LEVELS * OTHERS, ring_send.at[chunk], ring_recv.at[0, chunk]).wait_send()
+        for is_fused, levels in ((True, 3), (False, LEVELS)):
+            @pl.when((depth == 4) == is_fused)
+            def _():
+                whole(chunk, levels * OTHERS, ring_send.at[chunk], ring_recv.at[0, chunk]).wait_send()
+
+    @pl.when(depth == 3)
+    def _():
+        for level in range(2):
+            part = low.at[0, pl.ds(0, 8)]
+            remote(
+                part, part, pass_send.at[level], ring_recv.at[level, 0], device(child_a, row, core)
+            ).wait_send()
+
+    @pl.when(depth == 4)
+    def _():
+        for side in range(2):
+            part = low.at[:, pl.ds(0, 14)]
+            remote(
+                part, part, turn_send.at[side], turn_recv.at[0, side], device(leaf, row, 1 - core)
+            ).wait_send()
+        part = full.at[pl.ds(0, 7), own_half]
+        remote(
+            part, part, across_send.at[0], across_recv.at[0], device(leaf, row, 1 - core)
+        ).wait_send()
+
     whole(0, CHUNKS * OTHERS, red_send.at[0], red_recv.at[0, 0]).wait_send()
 
     @pl.when(has_upper)
@@ -292,7 +471,11 @@
             pltpu.VMEM((80, ROWS, 128), BF16),
             pltpu.VMEM((80, ROWS, 128), BF16),
             pltpu.VMEM((80, ROWS, 128), BF16),
+            pltpu.VMEM((CHUNKS, 16, ROWS, 128), BF16),
             pltpu.VMEM((2, CHUNKS, 16, ROWS, 128), BF16),
+            pltpu.VMEM((RING, 16, 128, 256), BF16),
+            pltpu.VMEM((2048, 256), BF16),
+            pltpu.VMEM((2048, 256), F32),
             dma((2, 3)),
             dma((2,)),
             dma((2,)),
@@ -303,6 +486,11 @@
             dma((CHUNKS,)),
             dma((LEVELS, CHUNKS)),
             dma((1,)),
+            dma((2,)),
+            dma((2,)),
+            dma((4, 2, 2)),
+            dma((1,)),
+            dma((5,)),
             pltpu.SemaphoreType.REGULAR,
         ],
         compiler_params=pltpu.CompilerParams(

time: 88.9 us -> 84.9 us (0.955)
  Pallas kernels: 87.9 us -> 84 us
    pallas_call x1, Pallas kernels: 87.9 us -> 84 us  [local(): pl.pallas_call(kernel, name='sweep', out_shape=pltpu.VMEM((2, 64, 256), F...]
where the time goes in v6:
time: 84.9 us; the launch traced here: 84.6 us
  Pallas kernels  84 us (99%)
    pallas_call x1, Pallas kernels, local(): pl.pallas_call(kernel, name='sweep', out_shape=pltpu.VMEM((2, 64, 256), F...  84 us

profile of v6, /device:TPU:2, one launch (start us, length us, event | category | flops | bytes accessed | tf_op | source)
XLA Modules:
  0.0 84.6 jit_solution(8169945134294550995)
XLA Ops:
  0.0 84.0 %sweep.1 = f32[2,64,256]{2,1,0:T(8,128)S(1)} custom-call(s32[2,16]{1,0:T(2,128)} %block_rows_in.1, f32[2,64,256]{2,1,0:T(8,128)} %right_side.1, bf16[2,2048,128]{2,1,0:T(8,128)(2,1)} %inverse_diag.1, bf16[2,16,128,256]{3,2,1,0:T(8,128)(2,1)} %lower_blocks.1), custom_call_target="tpu_custom_call" | custom-call | tf_op jit(solution)/shard_map/sweep/pallas_call | solution.py:459
  84.0 0.7 copy.6

commit v7 on v6

--- a/solution.py
+++ b/solution.py
@@ -291,10 +291,10 @@
     def _():
         own_low.start()
         halves[1].start()
+        loads[1, 2].wait()
+        start_turn()
         for chunk in range(CHUNKS):
             set_reduced(1, chunk, None)
-        loads[1, 2].wait()
-        start_turn()
         halves[0].start()
         wait_ready()
 

time: 84.9 us -> 84.5 us (level)
  no operation moved by 1% of the time
where the time goes in v7:
time: 84.5 us; the launch traced here: 84.4 us
  Pallas kernels  83.7 us (99%)
    pallas_call x1, Pallas kernels, local(): pl.pallas_call(kernel, name='sweep', out_shape=pltpu.VMEM((2, 64, 256), F...  83.7 us

profile of v7, /device:TPU:2, one launch (start us, length us, event | category | flops | bytes accessed | tf_op | source)
XLA Modules:
  0.0 84.4 jit_solution(5716382384491751253)
XLA Ops:
  0.0 83.7 %sweep.1 = f32[2,64,256]{2,1,0:T(8,128)S(1)} custom-call(s32[2,16]{1,0:T(2,128)} %block_rows_in.1, f32[2,64,256]{2,1,0:T(8,128)} %right_side.1, bf16[2,2048,128]{2,1,0:T(8,128)(2,1)} %inverse_diag.1, bf16[2,16,128,256]{3,2,1,0:T(8,128)(2,1)} %lower_blocks.1), custom_call_target="tpu_custom_call" | custom-call | tf_op jit(solution)/shard_map/sweep/pallas_call | solution.py:459
  83.7 0.7 copy.6

commit v8 on v7

--- a/solution.py
+++ b/solution.py
@@ -168,10 +168,16 @@
         def _():
             act(sibling, 0)
 
-    def spread(level, chunk):
+    def start_hops(level, chunk):
         each_hop(level, lambda where, which: hop(level, chunk, where, which).start())
+
+    def start_ring(level, chunk):
         for copy in ring_copies(level, chunk):
             copy.start()
+
+    def spread(level, chunk):
+        start_hops(level, chunk)
+        start_ring(level, chunk)
 
     own_half = pl.ds(8 * core, 8)
     quarters = (pl.ds(8 * core, 4), pl.ds(8 * core + 4, 4))
@@ -336,7 +342,8 @@
             def _():
                 for chunk in range(CHUNKS):
                     hop(level, chunk, leaf, 0).wait_recv()
-                    spread(level, chunk)
+                    start_ring(level, chunk)
+                    start_hops(level, chunk)
 
                 if level < 2:
                     @pl.when(depth == 3)
@@ -350,7 +357,8 @@
             def _():
                 for chunk in range(CHUNKS):
                     hop(level, chunk, leaf, 0).wait_recv()
-                    spread(level, chunk)
+                    start_ring(level, chunk)
+                    start_hops(level, chunk)
 
         @pl.when(depth == level)
         def _():
@@ -383,7 +391,9 @@
                 anc[chunk][16 * level + 2 * row + 1] = rounded[:, 128:]
                 if level == 0 and chunk == 0:
                     wait_ready()
-                spread(level, chunk)
+                start_hops(level, chunk)
+            for chunk in range(CHUNKS):
+                start_ring(level, chunk)
             if level == 0:
                 halves[0].start()
                 loads[1, 2].wait()

time: 84.5 us -> 83.4 us (0.987)
  Pallas kernels: 83.7 us -> 82.7 us
    pallas_call x1, Pallas kernels: 83.7 us -> 82.7 us  [local(): pl.pallas_call(kernel, name='sweep', out_shape=pltpu.VMEM((2, 64, 256), F...]
where the time goes in v8:
time: 83.4 us; the launch traced here: 83.3 us
  Pallas kernels  82.7 us (99%)
    pallas_call x1, Pallas kernels, local(): pl.pallas_call(kernel, name='sweep', out_shape=pltpu.VMEM((2, 64, 256), F...  82.7 us

profile of v8, /device:TPU:2, one launch (start us, length us, event | category | flops | bytes accessed | tf_op | source)
XLA Modules:
  0.0 83.3 jit_solution(7700301516414799772)
XLA Ops:
  0.0 82.7 %sweep.1 = f32[2,64,256]{2,1,0:T(8,128)S(1)} custom-call(s32[2,16]{1,0:T(2,128)} %block_rows_in.1, f32[2,64,256]{2,1,0:T(8,128)} %right_side.1, bf16[2,2048,128]{2,1,0:T(8,128)(2,1)} %inverse_diag.1, bf16[2,16,128,256]{3,2,1,0:T(8,128)(2,1)} %lower_blocks.1), custom_call_target="tpu_custom_call" | custom-call | tf_op jit(solution)/shard_map/sweep/pallas_call | solution.py:469
  82.7 0.7 copy.6

commit v9 on v8

--- a/solution.py
+++ b/solution.py
@@ -299,8 +299,6 @@
         halves[1].start()
         loads[1, 2].wait()
         start_turn()
-        for chunk in range(CHUNKS):
-            set_reduced(1, chunk, None)
         halves[0].start()
         wait_ready()
 
@@ -316,6 +314,8 @@
             def _():
                 if level == 0:
                     pass_turn(1)
+                    for chunk in range(CHUNKS):
+                        set_reduced(1, chunk, None)
                     wait_weights(1)
                     fuse(0)
                     pass_turn(2)

time: 83.4 us -> 84.1 us (level)
  no operation moved by 1% of the time
where the time goes in v9:
time: 84.1 us
  Pallas kernels  83.4 us (99%)
    pallas_call x1, Pallas kernels, local(): pl.pallas_call(kernel, name='sweep', out_shape=pltpu.VMEM((2, 64, 256), F...  83.4 us

profile of v9, /device:TPU:2, one launch (start us, length us, event | category | flops | bytes accessed | tf_op | source)
XLA Modules:
  0.0 84.1 jit_solution(10021472088532056410)
XLA Ops:
  0.0 83.4 %sweep.1 = f32[2,64,256]{2,1,0:T(8,128)S(1)} custom-call(s32[2,16]{1,0:T(2,128)} %block_rows_in.1, f32[2,64,256]{2,1,0:T(8,128)} %right_side.1, bf16[2,2048,128]{2,1,0:T(8,128)(2,1)} %inverse_diag.1, bf16[2,16,128,256]{3,2,1,0:T(8,128)(2,1)} %lower_blocks.1), custom_call_target="tpu_custom_call" | custom-call | tf_op jit(solution)/shard_map/sweep/pallas_call | solution.py:469
  83.4 0.7 copy.6
